TPU v7x, 32 devices: a whole 2x2x4 slice. The times are simulated.
32 devices in a mesh: dp: 16 (over z, y, core), fsdp: 2 (over x).
Axes of the slice: x: 2, y: 2, z: 4, core: 2. Of those that a mesh axis runs over, the one named last changes fastest.
Arguments:
- block_input: bfloat16 [32768, 768], P(('dp', 'fsdp')), may hold values from -6 to 6
- seq_long: int32 [16], P('dp'), may hold values 0 or 1
- ln1_gain: bfloat16 [768], P(('dp', 'fsdp')), may hold values from 0.099609375 to 1.8984375
- ln1_bias: bfloat16 [768], P(('dp', 'fsdp')), may hold values from -1.796875 to 1.796875
- w_qkv: bfloat16 [768, 2304], P(('dp', 'fsdp')), may hold values from -0.21875 to 0.21875
- b_qkv: bfloat16 [2304], P(('dp', 'fsdp')), may hold values from -1.796875 to 1.796875
- w_out: bfloat16 [768, 768], P(('dp', 'fsdp')), may hold values from -6 to 6
- b_out: bfloat16 [768], P(('dp', 'fsdp')), may hold values from -1.796875 to 1.796875
- ln2_gain: bfloat16 [768], P(('dp', 'fsdp')), may hold values from 0.099609375 to 1.8984375
- ln2_bias: bfloat16 [768], P(('dp', 'fsdp')), may hold values from -1.796875 to 1.796875
- w_fc: bfloat16 [768, 3072], P(('dp', 'fsdp')), may hold values from -0.21875 to 0.21875
- b_fc: bfloat16 [3072], P(('dp', 'fsdp')), may hold values from -1.796875 to 1.796875
- w_proj: bfloat16 [3072, 768], P(('dp', 'fsdp')), may hold values from -0.109375 to 0.109375
- b_proj: bfloat16 [768], P(('dp', 'fsdp')), may hold values from -1.796875 to 1.796875
- out_grad: bfloat16 [32768, 768], P(('dp', 'fsdp')), may hold values from -6 to 6
Outputs:
- block_output: bfloat16 [32768, 768], P(('dp', 'fsdp'))
- input_grad: float32 [32768, 768], P(('dp', 'fsdp'))
- grad_ln1_gain: float32 [768], P(('dp', 'fsdp'))
- grad_ln1_bias: float32 [768], P(('dp', 'fsdp'))
- grad_w_qkv: float32 [768, 2304], P(('dp', 'fsdp'))
- grad_b_qkv: float32 [2304], P(('dp', 'fsdp'))
- grad_w_out: float32 [768, 768], P(('dp', 'fsdp'))
- grad_b_out: float32 [768], P(('dp', 'fsdp'))
- grad_ln2_gain: float32 [768], P(('dp', 'fsdp'))
- grad_ln2_bias: float32 [768], P(('dp', 'fsdp'))
- grad_w_fc: float32 [768, 3072], P(('dp', 'fsdp'))
- grad_b_fc: float32 [3072], P(('dp', 'fsdp'))
- grad_w_proj: float32 [3072, 768], P(('dp', 'fsdp'))
- grad_b_proj: float32 [768], P(('dp', 'fsdp'))
Inputs may be any that keep to these rules, and one draw needn't show every extreme that they name: `seq_long`: 0 or 1 for each group of 2048 tokens.
All inputs are finite; a program needn't handle non-finite values.
Results may differ from a plain program's by a relative error of at most 0.0098.
Values may be sent and summed in bfloat16 or wider, within the bound.
No kernel may reach another device: no remote copies, remote signals or barrier semaphores. Data moves between devices by JAX's collectives and lax.ppermute only.
A program may use at most 256 MiB of HBM per device.

v0:
```python
import functools
import math

import jax
import jax.numpy as jnp
from jax import lax
from jax.experimental import pallas as pl
from jax.experimental.pallas import tpu as pltpu
from jax.sharding import PartitionSpec as P


f32 = jnp.float32
bf = jnp.bfloat16


D = 768
HEADS = 12
HD = 64
FF = 3072
SEQ = 1024


EPS = 1e-05
FAR = -1e30


def layer_norm(rows_in, gain_vec, bias_vec):
    row_mean = jnp.mean(rows_in, axis=-1, keepdims=True)
    centred = rows_in - row_mean
    variance = jnp.mean(centred * centred, axis=-1, keepdims=True)
    return centred * lax.rsqrt(variance + EPS) * gain_vec + bias_vec


def product(left, right):
    return jnp.dot(left, right, preferred_element_type=jnp.float32)


def product_tn(left, right):
    return lax.dot_general(
        left, right, (((0,), (0,)), ((), ())), preferred_element_type=jnp.float32
    )


def product_nt(left, right):
    return lax.dot_general(
        left, right, (((1,), (1,)), ((), ())), preferred_element_type=jnp.float32
    )


def gather_first(kv_rows):
    return lax.all_gather(kv_rows, "fsdp", axis=0, tiled=True)


def gather_second(kv_rows):
    return lax.all_gather(kv_rows, "fsdp", axis=0, tiled=True)


def block_layout(kv_all):
    group_rows = kv_all.shape[0]
    key_block = math.gcd(group_rows, 512)
    block_count = group_rows // key_block
    kv_blocks = kv_all.reshape(block_count, key_block, 2, HEADS, HD)
    return (key_block, kv_blocks, jnp.arange(block_count, dtype=jnp.int32))


def block_allowed(query_pos, key_start, key_block, seq_length):
    key_pos = key_start + jnp.arange(key_block, dtype=jnp.int32)
    return (query_pos[:, None] // seq_length == key_pos[None, :] // seq_length) & (
        key_pos[None, :] <= query_pos[:, None]
    )


def block_useful(key_start, key_block, query_pos, first_valid):
    return (key_start <= query_pos[-1]) & (key_start + key_block - 1 >= first_valid)


def score_parts(queries, key_part):
    scores = jnp.einsum(
        "qhd,khd->hqk", queries, key_part, preferred_element_type=jnp.float32
    ) * HD ** (-0.5)
    return (scores, jnp.sqrt(scores * scores + 1.0))


def attend(queries, kv_all, query_pos, seq_length, first_valid):
    key_block, kv_blocks, block_ids = block_layout(kv_all)
    row_total = queries.shape[0]

    def stats_step(state_now, block_item):
        block_id, kv_part = block_item
        key_start = block_id * key_block

        def stats_compute(state_in):
            row_top, row_sum = state_in
            allowed = block_allowed(query_pos, key_start, key_block, seq_length)[None]
            _, magnitude = score_parts(queries, kv_part[:, 0])
            masked = jnp.where(allowed, magnitude, FAR)
            new_top = jnp.maximum(row_top, jnp.max(masked, axis=-1))
            fresh = jnp.sum(jnp.where(allowed, jnp.exp(masked - new_top[:, :, None]), 0.0), axis=-1)
            return (new_top, row_sum * jnp.exp(row_top - new_top) + fresh)

        useful = block_useful(key_start, key_block, query_pos, first_valid)
        return (lax.cond(useful, stats_compute, lambda kept_state: kept_state, state_now), None)

    start_state = (
        jnp.full((HEADS, row_total), FAR, jnp.float32),
        jnp.zeros((HEADS, row_total), jnp.float32),
    )
    (row_top, row_sum), unused = lax.scan(stats_step, start_state, (block_ids, kv_blocks))
    log_total = row_top + jnp.log(row_sum)

    def value_step(accum_now, block_item):
        block_id, kv_part = block_item
        key_start = block_id * key_block

        def value_compute(accum_in):
            allowed = block_allowed(query_pos, key_start, key_block, seq_length)[None]
            scores, magnitude = score_parts(queries, kv_part[:, 0])
            weights = jnp.where(
                allowed, jnp.tanh(scores) * jnp.exp(magnitude - log_total[:, :, None]), 0.0
            ).astype(jnp.bfloat16)
            return accum_in + jnp.einsum(
                "hqk,khd->qhd", weights, kv_part[:, 1], preferred_element_type=jnp.float32
            )

        useful = block_useful(key_start, key_block, query_pos, first_valid)
        return (lax.cond(useful, value_compute, lambda kept_accum: kept_accum, accum_now), None)

    start_accum = jnp.zeros((row_total, HEADS, HD), jnp.float32)
    attn_heads, unused = lax.scan(value_step, start_accum, (block_ids, kv_blocks))
    return (attn_heads, log_total)


def attend_back(
    queries, kv_all, query_pos, seq_length, first_valid, log_total, attn_heads, grad_heads
):
    key_block, kv_blocks, block_ids = block_layout(kv_all)
    row_total = queries.shape[0]
    inner = jnp.transpose(jnp.sum(grad_heads.astype(jnp.float32) * attn_heads, axis=-1))

    def grad_step(dq_now, block_item):
        block_id, kv_part = block_item
        key_start = block_id * key_block

        def grad_compute(dq_in):
            allowed = block_allowed(query_pos, key_start, key_block, seq_length)[None]
            scores, magnitude = score_parts(queries, kv_part[:, 0])
            expo = jnp.where(allowed, jnp.exp(magnitude - log_total[:, :, None]), 0.0)
            tangent = jnp.tanh(scores)
            weights = (tangent * expo).astype(jnp.bfloat16)
            grad_v = jnp.einsum(
                "hqk,qhd->khd", weights, grad_heads, preferred_element_type=jnp.float32
            )
            grad_weight = jnp.einsum(
                "qhd,khd->hqk", grad_heads, kv_part[:, 1], preferred_element_type=jnp.float32
            )
            slope = scores / magnitude
            grad_scores = (
                expo
                * (
                    grad_weight * (1.0 - tangent * tangent + tangent * slope)
                    - slope * inner[:, :, None]
                )
            ).astype(jnp.bfloat16)
            dq_out = dq_in + jnp.einsum(
                "hqk,khd->qhd", grad_scores, kv_part[:, 0], preferred_element_type=jnp.float32
            ) * HD ** (-0.5)
            grad_k = jnp.einsum(
                "hqk,qhd->khd", grad_scores, queries, preferred_element_type=jnp.float32
            ) * HD ** (-0.5)
            return (
                dq_out,
                jnp.concatenate(
                    [grad_k.reshape(key_block, D), grad_v.reshape(key_block, D)], axis=1
                ),
            )

        def skip_block(dq_in):
            return (dq_in, jnp.zeros((key_block, 2 * D), jnp.float32))

        useful = block_useful(key_start, key_block, query_pos, first_valid)
        return lax.cond(useful, grad_compute, skip_block, dq_now)

    start_dq = jnp.zeros((row_total, HEADS, HD), jnp.float32)
    grad_q, kv_grads = lax.scan(grad_step, start_dq, (block_ids, kv_blocks))
    return (grad_q, kv_grads.reshape(kv_all.shape[0], 2 * D))


def forward(block_input, weight_set, long_flag, fsdp_index, gather_keys):
    (
        ln1_gain,
        ln1_bias,
        w_qkv,
        b_qkv,
        w_out,
        b_out,
        ln2_gain,
        ln2_bias,
        w_fc,
        b_fc,
        w_proj,
        b_proj,
    ) = weight_set
    row_total = block_input.shape[0]
    wide_input = block_input.astype(jnp.float32)
    normed_one = layer_norm(
        wide_input, ln1_gain.astype(jnp.float32), ln1_bias.astype(jnp.float32)
    ).astype(jnp.bfloat16)
    projected = (product(normed_one, w_qkv) + b_qkv.astype(jnp.float32)).astype(jnp.bfloat16)
    queries = projected[:, :D].reshape(row_total, HEADS, HD)
    kv_all = gather_keys(projected[:, D:])
    seq_length = jnp.where(long_flag == 1, 2 * SEQ, SEQ).astype(jnp.int32)
    query_pos = fsdp_index * row_total + jnp.arange(row_total, dtype=jnp.int32)
    first_valid = query_pos[0] // seq_length * seq_length
    attn_heads, log_total = attend(queries, kv_all, query_pos, seq_length, first_valid)
    mixed = attn_heads.reshape(row_total, D).astype(jnp.bfloat16)
    middle = wide_input + product(mixed, w_out) + b_out.astype(jnp.float32)
    normed_two = layer_norm(
        middle, ln2_gain.astype(jnp.float32), ln2_bias.astype(jnp.float32)
    ).astype(jnp.bfloat16)
    hidden_pre = product(normed_two, w_fc) + b_fc.astype(jnp.float32)
    hidden_act = jax.nn.gelu(hidden_pre).astype(jnp.bfloat16)
    block_out = middle + product(hidden_act, w_proj) + b_proj.astype(jnp.float32)
    return (
        block_out,
        normed_one,
        queries,
        kv_all,
        query_pos,
        seq_length,
        first_valid,
        attn_heads,
        log_total,
        mixed,
        middle,
        normed_two,
        hidden_pre,
        hidden_act,
    )


def backward(saved, weight_set, block_input, out_grad):
    (
        _,
        normed_one,
        queries,
        kv_all,
        query_pos,
        seq_length,
        first_valid,
        attn_heads,
        log_total,
        mixed,
        middle,
        normed_two,
        hidden_pre,
        hidden_act,
    ) = saved
    (ln1_gain, ln1_bias, w_qkv, _, w_out, _, ln2_gain, ln2_bias, w_fc, _, w_proj, _) = weight_set
    row_total = block_input.shape[0]
    grad_out = out_grad.astype(jnp.float32)
    grad_w_proj = product_tn(hidden_act, out_grad)
    grad_b_proj = jnp.sum(grad_out, axis=0)
    grad_act = product_nt(out_grad, w_proj)
    unused, gelu_pull = jax.vjp(jax.nn.gelu, hidden_pre)
    grad_pre = gelu_pull(grad_act)[0].astype(jnp.bfloat16)
    grad_w_fc = product_tn(normed_two, grad_pre)
    grad_b_fc = jnp.sum(grad_pre.astype(jnp.float32), axis=0)
    unused, norm_pull_two = jax.vjp(
        layer_norm, middle, ln2_gain.astype(jnp.float32), ln2_bias.astype(jnp.float32)
    )
    grad_mid_norm, grad_ln2_gain, grad_ln2_bias = norm_pull_two(product_nt(grad_pre, w_fc))
    grad_middle = grad_out + grad_mid_norm
    grad_mid_low = grad_middle.astype(jnp.bfloat16)
    grad_w_out = product_tn(mixed, grad_mid_low)
    grad_b_out = jnp.sum(grad_mid_low.astype(jnp.float32), axis=0)
    grad_heads = product_nt(grad_mid_low, w_out).astype(jnp.bfloat16).reshape(row_total, HEADS, HD)
    grad_q, kv_grads = attend_back(
        queries, kv_all, query_pos, seq_length, first_valid, log_total, attn_heads, grad_heads
    )
    kv_mine = lax.psum_scatter(
        kv_grads.astype(jnp.bfloat16), "fsdp", scatter_dimension=0, tiled=True
    ).astype(jnp.float32)
    grad_proj = jnp.concatenate([grad_q.reshape(row_total, D), kv_mine], axis=1).astype(
        jnp.bfloat16
    )
    grad_w_qkv = product_tn(normed_one, grad_proj)
    grad_b_qkv = jnp.sum(grad_proj.astype(jnp.float32), axis=0)
    unused, norm_pull_one = jax.vjp(
        layer_norm,
        block_input.astype(jnp.float32),
        ln1_gain.astype(jnp.float32),
        ln1_bias.astype(jnp.float32),
    )
    grad_in_norm, grad_ln1_gain, grad_ln1_bias = norm_pull_one(product_nt(grad_proj, w_qkv))
    input_grad = grad_middle + grad_in_norm
    grad_set = (
        grad_ln1_gain,
        grad_ln1_bias,
        grad_w_qkv,
        grad_b_qkv,
        grad_w_out,
        grad_b_out,
        grad_ln2_gain,
        grad_ln2_bias,
        grad_w_fc,
        grad_b_fc,
        grad_w_proj,
        grad_b_proj,
    )
    return (input_grad, grad_set)


def on_device_generic(
    block_input,
    seq_long,
    ln1_gain,
    ln1_bias,
    w_qkv,
    b_qkv,
    w_out,
    b_out,
    ln2_gain,
    ln2_bias,
    w_fc,
    b_fc,
    w_proj,
    b_proj,
    out_grad,
):
    long_flag = seq_long[0]
    fsdp_index = lax.axis_index("fsdp")
    weight_set = (
        lax.all_gather(ln1_gain, ("dp", "fsdp"), axis=0, tiled=True),
        lax.all_gather(ln1_bias, ("dp", "fsdp"), axis=0, tiled=True),
        lax.all_gather(w_qkv, ("dp", "fsdp"), axis=0, tiled=True),
        lax.all_gather(b_qkv, ("dp", "fsdp"), axis=0, tiled=True),
        lax.all_gather(w_out, ("dp", "fsdp"), axis=0, tiled=True),
        lax.all_gather(b_out, ("dp", "fsdp"), axis=0, tiled=True),
        lax.all_gather(ln2_gain, ("dp", "fsdp"), axis=0, tiled=True),
        lax.all_gather(ln2_bias, ("dp", "fsdp"), axis=0, tiled=True),
        lax.all_gather(w_fc, ("dp", "fsdp"), axis=0, tiled=True),
        lax.all_gather(b_fc, ("dp", "fsdp"), axis=0, tiled=True),
        lax.all_gather(w_proj, ("dp", "fsdp"), axis=0, tiled=True),
        lax.all_gather(b_proj, ("dp", "fsdp"), axis=0, tiled=True),
    )
    saved = forward(block_input, weight_set, long_flag, fsdp_index, gather_first)
    block_output = saved[0].astype(jnp.bfloat16)
    weight_set = (
        lax.all_gather(ln1_gain, ("dp", "fsdp"), axis=0, tiled=True),
        lax.all_gather(ln1_bias, ("dp", "fsdp"), axis=0, tiled=True),
        lax.all_gather(w_qkv, ("dp", "fsdp"), axis=0, tiled=True),
        lax.all_gather(b_qkv, ("dp", "fsdp"), axis=0, tiled=True),
        lax.all_gather(w_out, ("dp", "fsdp"), axis=0, tiled=True),
        lax.all_gather(b_out, ("dp", "fsdp"), axis=0, tiled=True),
        lax.all_gather(ln2_gain, ("dp", "fsdp"), axis=0, tiled=True),
        lax.all_gather(ln2_bias, ("dp", "fsdp"), axis=0, tiled=True),
        lax.all_gather(w_fc, ("dp", "fsdp"), axis=0, tiled=True),
        lax.all_gather(b_fc, ("dp", "fsdp"), axis=0, tiled=True),
        lax.all_gather(w_proj, ("dp", "fsdp"), axis=0, tiled=True),
        lax.all_gather(b_proj, ("dp", "fsdp"), axis=0, tiled=True),
    )
    saved = forward(block_input, weight_set, long_flag, fsdp_index, gather_second)
    input_grad, grad_set = backward(saved, weight_set, block_input, out_grad)
    grad_shards = (
        lax.psum_scatter(grad_set[0], ("dp", "fsdp"), scatter_dimension=0, tiled=True),
        lax.psum_scatter(grad_set[1], ("dp", "fsdp"), scatter_dimension=0, tiled=True),
        lax.psum_scatter(grad_set[2], ("dp", "fsdp"), scatter_dimension=0, tiled=True),
        lax.psum_scatter(grad_set[3], ("dp", "fsdp"), scatter_dimension=0, tiled=True),
        lax.psum_scatter(grad_set[4], ("dp", "fsdp"), scatter_dimension=0, tiled=True),
        lax.psum_scatter(grad_set[5], ("dp", "fsdp"), scatter_dimension=0, tiled=True),
        lax.psum_scatter(grad_set[6], ("dp", "fsdp"), scatter_dimension=0, tiled=True),
        lax.psum_scatter(grad_set[7], ("dp", "fsdp"), scatter_dimension=0, tiled=True),
        lax.psum_scatter(grad_set[8], ("dp", "fsdp"), scatter_dimension=0, tiled=True),
        lax.psum_scatter(grad_set[9], ("dp", "fsdp"), scatter_dimension=0, tiled=True),
        lax.psum_scatter(grad_set[10], ("dp", "fsdp"), scatter_dimension=0, tiled=True),
        lax.psum_scatter(grad_set[11], ("dp", "fsdp"), scatter_dimension=0, tiled=True),
    )
    return (block_output, input_grad) + tuple(grad_shards)


def nt(a, b):
    return lax.dot_general(a, b, (((1,), (1,)), ((), ())), preferred_element_type=f32)


def nn(a, b):
    return jnp.dot(a, b, preferred_element_type=f32)


PAIR = 2 * HD


def busy(microseconds):
    return pl.CostEstimate(
        flops=int(microseconds * 1.15e9), bytes_accessed=int(microseconds * 1e6), transcendentals=0
    )


def split_heads(pair):
    left = lax.broadcasted_iota(jnp.int32, pair.shape, 1) < HD
    zero = jnp.zeros_like(pair)
    return (jnp.where(left, pair, zero), jnp.where(left, zero, pair))


def up_to(keys, queries):
    return lax.broadcasted_iota(jnp.int32, (keys, queries), 0) <= lax.broadcasted_iota(
        jnp.int32, (keys, queries), 1
    )


def attend_fwd_kernel(block, strips, flag_ref, q_ref, k_ref, v_ref, o_ref, lse_ref, vt_ref):
    i = pl.program_id(0)
    part = block // strips

    @pl.when(i == 0)
    def _():
        vt_ref[...] = v_ref[...].astype(f32).T.astype(bf)

    per_seq = jnp.where(flag_ref[0] == 1, 2 * SEQ, SEQ) // block
    first = i // per_seq * per_seq
    q_heads = split_heads(q_ref[...])

    def update(state, h, start, keys, low, mask):
        start = pl.multiple_of(start, part)
        s = nt(k_ref[pl.ds(start, keys), :], q_heads[h][low:, :])
        x = s * s + 1.0
        mag = x * lax.rsqrt(x)
        if mask is not None:
            mag = jnp.where(mask, mag, FAR)
        top = jnp.max(mag, axis=0, keepdims=True)
        if state is not None:
            old_top, old_sum, old_acc = state
            top = jnp.maximum(top, old_top)
        e = jnp.exp(mag - top)
        fresh = jnp.sum(e, axis=0, keepdims=True)
        w = (jnp.tanh(s) * e).astype(bf)
        acc = nn(vt_ref[h * HD : (h + 1) * HD, pl.ds(start, keys)], w)
        if state is not None:
            alpha = jnp.exp(old_top - top)
            fresh = fresh + alpha * old_sum
            acc = acc + alpha * old_acc
        return (top, fresh, acc)

    base = i * block
    states = []
    for h in range(2):
        state = update(None, h, base, part, 0, up_to(part, block))
        for m in range(1, strips):
            low = m * part
            tail = update(
                tuple(item[:, low:] for item in state),
                h,
                base + low,
                part,
                low,
                up_to(part, block - low),
            )
            state = tuple(
                jnp.concatenate([a[:, :low], b], axis=1) for a, b in zip(state, tail)
            )
        states.append(state)
    states = lax.fori_loop(
        first,
        i,
        lambda j, st: tuple(update(st[h], h, j * block, block, 0, None) for h in range(2)),
        tuple(states),
    )
    for h in range(2):
        top, total, _ = states[h]
        lse_ref[h : h + 1, :] = top + jnp.log(total)
    both = jnp.concatenate([states[h][2] / states[h][1] for h in range(2)], axis=0)
    o_ref[...] = both.T.astype(bf)


def attend_fwd(flag, projected, pair, block=1024, strips=4):
    rows = projected.shape[0]
    full = lambda c: pl.BlockSpec((rows, PAIR), lambda i, f: (0, 3 * pair + c))
    return pl.pallas_call(
        functools.partial(attend_fwd_kernel, block, strips),
        grid_spec=pltpu.PrefetchScalarGridSpec(
            num_scalar_prefetch=1,
            grid=(rows // block,),
            in_specs=[pl.BlockSpec((block, PAIR), lambda i, f: (i, 3 * pair)), full(1), full(2)],
            out_specs=[
                pl.BlockSpec((block, PAIR), lambda i, f: (i, 0)),
                pl.BlockSpec((8, block), lambda i, f: (0, i)),
            ],
            scratch_shapes=[pltpu.VMEM((PAIR, rows), bf)],
        ),
        out_shape=[
            jax.ShapeDtypeStruct((rows, PAIR), bf),
            jax.ShapeDtypeStruct((8, rows), f32),
        ],
        cost_estimate=busy(16),
        name="attend_fwd",
    )(flag, projected, projected, projected)


def attend_bwd_kernel(
    block,
    strips,
    flag_ref,
    place_ref,
    q_ref,
    k_ref,
    v_ref,
    o_ref,
    keep_ref,
    other_ref,
    lse_ref,
    g_ref,
    dqt_ref,
    inner_ref,
    do_ref,
):
    j = pl.program_id(0)
    last = pl.num_programs(0) - 1
    rows = q_ref.shape[0]
    side_rows = rows // 2
    part = block // strips

    @pl.when(j == 0)
    def _():
        dqt_ref[...] = jnp.zeros_like(dqt_ref)
        on_left = place_ref[0] == 0
        do_ref[:side_rows, :] = jnp.where(on_left, keep_ref[...], other_ref[...])
        do_ref[side_rows:, :] = jnp.where(on_left, other_ref[...], keep_ref[...])
        prod = o_ref[...].astype(f32) * do_ref[...].astype(f32)
        head = lax.broadcasted_iota(jnp.int32, (8, PAIR), 0)
        lane = lax.broadcasted_iota(jnp.int32, (8, PAIR), 1)
        inner_ref[...] = lax.dot_general(
            (head == lane // HD).astype(f32),
            prod,
            (((1,), (1,)), ((), ())),
            precision=lax.Precision.HIGHEST,
            preferred_element_type=f32,
        )

    per_seq = jnp.where(flag_ref[0] == 1, 2 * SEQ, SEQ) // block
    stop = (j // per_seq + 1) * per_seq
    k_pair = k_ref[...]
    k_heads = split_heads(k_pair)
    v_heads = split_heads(v_ref[...])
    k_turned = k_pair.astype(f32).T.astype(bf)

    def update(state, low_key, keys, start, queries, mask):
        cols = pl.ds(pl.multiple_of(start, part), queries)
        q_pair = q_ref[cols, :]
        do_pair = do_ref[cols, :]
        q_heads = split_heads(q_pair)
        do_heads = split_heads(do_pair)
        key_rows = slice(low_key, low_key + keys)
        dk, dv = (None, None) if state is None else state
        for h in range(2):
            head_rows = slice(h * HD, (h + 1) * HD)
            s = nt(k_heads[h][key_rows], q_pair)
            x = s * s + 1.0
            r = lax.rsqrt(x)
            e = jnp.exp(x * r - lse_ref[h : h + 1, cols])
            if mask is not None:
                e = jnp.where(mask, e, 0.0)
            t = jnp.tanh(s)
            slope = s * r
            w = (t * e).astype(bf)
            gw = nt(v_heads[h][key_rows], do_pair)
            ds = (
                e * (gw * (1.0 + t * (slope - t)) - slope * inner_ref[h : h + 1, cols])
            ).astype(bf)
            dv_part = nn(w, do_heads[h])
            dk_part = nn(ds, q_heads[h])
            dv = dv_part if dv is None else dv + dv_part
            dk = dk_part if dk is None else dk + dk_part
            dqt_ref[head_rows, cols] += nn(k_turned[head_rows, key_rows], ds)
        return (dk, dv)

    base = j * block
    strip_grads = [
        update(None, m * part, part, base + m * part, block - m * part, up_to(part, block - m * part))
        for m in range(strips)
    ]
    state = tuple(jnp.concatenate(items, axis=0) for items in zip(*strip_grads))
    dk, dv = lax.fori_loop(
        j + 1, stop, lambda i, st: update(st, 0, block, i * block, block, None), state
    )
    mine = pl.ds(pl.multiple_of(base, block), block)
    g_ref[mine, PAIR : 2 * PAIR] = dk.astype(bf)
    g_ref[mine, 2 * PAIR :] = dv.astype(bf)

    @pl.when(j == last)
    def _():
        g_ref[:, :PAIR] = (dqt_ref[...] * HD**-0.5).T.astype(bf)


def attend_bwd(flag, place, projected, pair, heads_out, keep, other, lse, block=1024, strips=4):
    rows = projected.shape[0]
    fixed = lambda r: pl.BlockSpec((r, PAIR), lambda j, f, s: (0, 0))
    part = lambda c: pl.BlockSpec((block, PAIR), lambda j, f, s: (j, 3 * pair + c))
    return pl.pallas_call(
        functools.partial(attend_bwd_kernel, block, strips),
        grid_spec=pltpu.PrefetchScalarGridSpec(
            num_scalar_prefetch=2,
            grid=(rows // block,),
            in_specs=[
                pl.BlockSpec((rows, PAIR), lambda j, f, s: (0, 3 * pair)),
                part(1),
                part(2),
                fixed(rows),
                fixed(rows // 2),
                fixed(rows // 2),
                pl.BlockSpec((8, rows), lambda j, f, s: (0, 0)),
            ],
            out_specs=pl.BlockSpec((rows, 3 * PAIR), lambda j, f, s: (0, 0)),
            scratch_shapes=[
                pltpu.VMEM((PAIR, rows), f32),
                pltpu.VMEM((8, rows), f32),
                pltpu.VMEM((rows, PAIR), bf),
            ],
        ),
        out_shape=jax.ShapeDtypeStruct((rows, 3 * PAIR), bf),
        cost_estimate=busy(25),
        name="attend_bwd",
    )(flag, place, projected, projected, projected, heads_out, keep, other, lse)


def tn(a, b):
    return lax.dot_general(a, b, (((0,), (0,)), ((), ())), preferred_element_type=f32)


def norm_stats(rows_in):
    mean = jnp.mean(rows_in, axis=-1, keepdims=True)
    centred = rows_in - mean
    variance = jnp.mean(centred * centred, axis=-1, keepdims=True)
    scale = lax.rsqrt(variance + EPS)
    return centred * scale, scale


def project_kernel(place_ref, own_ref, other_ref, gain_ref, bias_ref, w_ref, b_ref, n_ref, p_ref):
    per_side = pl.num_programs(0) // 2
    is_own = pl.program_id(0) // per_side == place_ref[0]
    rows = jnp.where(is_own, own_ref[...], other_ref[...]).astype(f32)
    unit, _ = norm_stats(rows)
    normed = (unit * gain_ref[...] + bias_ref[...]).astype(bf)
    n_ref[...] = normed
    for c in range(0, p_ref.shape[1], 3 * PAIR):
        cols = slice(c, c + 3 * PAIR)
        part = (nn(normed, w_ref[:, cols]) + b_ref[:, cols]).astype(bf)
        p_ref[:, c : c + PAIR] = part[:, :PAIR] * jnp.asarray(HD**-0.5, bf)
        p_ref[:, c + PAIR : c + 3 * PAIR] = part[:, PAIR:]


def project(place, own, other, gain, bias, weight, w_bias, block=256):
    rows, width = own.shape
    per_side = rows // block
    cols = weight.shape[1]
    fixed = lambda shape: pl.BlockSpec(shape, lambda i, s: (0, 0))
    return pl.pallas_call(
        project_kernel,
        grid_spec=pltpu.PrefetchScalarGridSpec(
            num_scalar_prefetch=1,
            grid=(2 * per_side,),
            in_specs=[
                pl.BlockSpec(
                    (block, width), lambda i, s: (jnp.clip(i - s[0] * per_side, 0, per_side - 1), 0)
                ),
                pl.BlockSpec(
                    (block, width),
                    lambda i, s: (jnp.clip(i - (1 - s[0]) * per_side, 0, per_side - 1), 0),
                ),
                fixed((1, width)),
                fixed((1, width)),
                fixed(weight.shape),
                fixed((1, cols)),
            ],
            out_specs=[
                pl.BlockSpec((block, width), lambda i, s: (i, 0)),
                pl.BlockSpec((block, cols), lambda i, s: (i, 0)),
            ],
        ),
        out_shape=[
            jax.ShapeDtypeStruct((2 * rows, width), bf),
            jax.ShapeDtypeStruct((2 * rows, cols), bf),
        ],
        cost_estimate=busy(11),
        name="norm_project",
    )(place, own, other, gain, bias, weight, w_bias)


GELU_C = math.sqrt(2 / math.pi)


def mlp_kernel(
    place_ref,
    g_hbm,
    x_ref,
    og_ref,
    ha0_ref,
    ha1_ref,
    ha2_ref,
    hb0_ref,
    hb1_ref,
    hb2_ref,
    bout_ref,
    gain_ref,
    bias_ref,
    bfc_ref,
    bproj_ref,
    out_ref,
    mixed_ref,
    n2_ref,
    act_ref,
    gp_ref,
    gm_ref,
    gml_ref,
    keep0_ref,
    keep1_ref,
    keep2_ref,
    send0_ref,
    send1_ref,
    send2_ref,
    sums_ref,
    w_ref,
    sem,
):
    i = pl.program_id(0)
    devices = g_hbm.shape[0]
    sub = g_hbm.shape[2]
    width = devices * sub
    chunks = (g_hbm.shape[1] - 1) // 2

    def load(slot):
        return pltpu.make_async_copy(g_hbm.at[:, slot], w_ref.at[slot], sem.at[slot])

    order = [2 * chunks] + list(range(chunks, 2 * chunks))

    def load_proj():
        return pltpu.make_async_copy(
            g_hbm.at[:, pl.ds(0, chunks)], wp_view(), sem.at[0]
        )

    def wp_view():
        return w_ref.at[pl.ds(0, chunks)].reshape(devices, chunks, sub, width)

    @pl.when(i == 0)
    def _():
        for slot in order:
            load(slot).start()
        load_proj().start()
        for slot in order:
            load(slot).wait()
        load_proj().wait()
        sums_ref[...] = jnp.zeros_like(sums_ref)

    def weight(slot):
        return w_ref[slot].reshape(width, width)

    on_left = place_ref[0] == 0
    ha = jnp.concatenate([ha0_ref[...], ha1_ref[...], ha2_ref[...]], axis=1)
    hb = jnp.concatenate([hb0_ref[...], hb1_ref[...], hb2_ref[...]], axis=1)
    mixed = jnp.concatenate([jnp.where(on_left, ha, hb), jnp.where(on_left, hb, ha)], axis=1)
    mixed_ref[...] = mixed
    og_low = og_ref[...]
    og = og_low.astype(f32)
    middle = x_ref[...].astype(f32) + nn(mixed, weight(2 * chunks)) + bout_ref[...]
    unit, scale = norm_stats(middle)
    n2 = (unit * gain_ref[...] + bias_ref[...]).astype(bf)
    n2_ref[...] = n2
    out = middle + bproj_ref[...]
    e = jnp.zeros_like(middle)
    for c in range(chunks):
        cols = slice(c * width, (c + 1) * width)
        w_fc = weight(chunks + c)
        w_proj = weight(c)
        pre = nn(n2, w_fc) + bfc_ref[:, cols]
        square = pre * pre
        t = jnp.tanh(GELU_C * pre * (1.0 + 0.044715 * square))
        low_half = 0.5 * (1.0 + t)
        act = (pre * low_half).astype(bf)
        act_ref[:, cols] = act
        out = out + nn(act, w_proj)
        slope = low_half + 0.5 * pre * (1.0 - t * t) * (
            GELU_C * (1.0 + 3.0 * 0.044715 * square)
        )
        gp = (nt(og_low, w_proj) * slope).astype(bf)
        gp_ref[:, cols] = gp
        sums_ref[0:1, cols] += jnp.sum(gp.astype(f32), axis=0, keepdims=True)
        e = e + nt(gp, w_fc)
    out_ref[...] = out.astype(bf)
    sums_ref[1:2, 0:width] += jnp.sum(og, axis=0, keepdims=True)
    sums_ref[1:2, width : 2 * width] += jnp.sum(e * unit, axis=0, keepdims=True)
    sums_ref[1:2, 2 * width : 3 * width] += jnp.sum(e, axis=0, keepdims=True)
    eg = e * gain_ref[...]
    gm = og + scale * (
        eg
        - jnp.mean(eg, axis=-1, keepdims=True)
        - unit * jnp.mean(eg * unit, axis=-1, keepdims=True)
    )
    gm_ref[...] = gm
    gml = gm.astype(bf)
    gml_ref[...] = gml
    sums_ref[1:2, 3 * width : 4 * width] += jnp.sum(gml.astype(f32), axis=0, keepdims=True)
    gh = nt(gml, weight(2 * chunks)).astype(bf)
    half = width // 2
    left = gh[:, :half]
    right = gh[:, half:]
    for p, (keep_ref, send_ref) in enumerate(
        ((keep0_ref, send0_ref), (keep1_ref, send1_ref), (keep2_ref, send2_ref))
    ):
        cols = slice(p * PAIR, (p + 1) * PAIR)
        keep_ref[...] = jnp.where(on_left, left[:, cols], right[:, cols])
        send_ref[...] = jnp.where(on_left, right[:, cols], left[:, cols])


def mlp(place, gathered, x, og, heads_mine, heads_other, b_out, gain, bias, b_fc, b_proj, block=256):
    rows, width = x.shape
    steps = rows // block
    hidden = b_fc.shape[1]
    row = lambda cols: pl.BlockSpec((block, cols), lambda i, s: (i, 0))
    fixed = lambda cols: pl.BlockSpec((1, cols), lambda i, s: (0, 0))
    shape = lambda cols, kind: jax.ShapeDtypeStruct((rows, cols), kind)
    return pl.pallas_call(
        mlp_kernel,
        grid_spec=pltpu.PrefetchScalarGridSpec(
            num_scalar_prefetch=1,
            grid=(steps,),
            in_specs=[
                pl.BlockSpec(memory_space=pl.ANY),
                row(width),
                row(width),
                *[pl.BlockSpec((block, PAIR), lambda i, s: (s[0] * steps + i, 0))] * 3,
                *[row(PAIR)] * 3,
                fixed(width),
                fixed(width),
                fixed(width),
                fixed(hidden),
                fixed(width),
            ],
            out_specs=[
                row(width),
                row(width),
                row(width),
                row(hidden),
                row(hidden),
                row(width),
                row(width),
                *[row(PAIR)] * 6,
                pl.BlockSpec((8, hidden), lambda i, s: (0, 0)),
            ],
            scratch_shapes=[
                pltpu.VMEM((gathered.shape[1], gathered.shape[0], gathered.shape[2], width), bf),
                pltpu.SemaphoreType.DMA((gathered.shape[1],)),
            ],
        ),
        out_shape=[
            shape(width, bf),
            shape(width, bf),
            shape(width, bf),
            shape(hidden, bf),
            shape(hidden, bf),
            shape(width, f32),
            shape(width, bf),
            *[shape(PAIR, bf)] * 6,
            jax.ShapeDtypeStruct((8, hidden), f32),
        ],
        compiler_params=pltpu.CompilerParams(vmem_limit_bytes=56 * 1024 * 1024),
        cost_estimate=busy(37),
        name="mlp",
    )(place, gathered, x, og, *heads_mine, *heads_other, b_out, gain, bias, b_fc, b_proj)


def weight_grad_kernel(act_ref, gp_ref, og_ref, n2_ref, mixed_ref, gml_ref, out_hbm, buf_ref, sem):
    c = pl.program_id(0)
    last = pl.num_programs(0) - 1
    devices, slots, sub, width = out_hbm.shape
    chunks = (slots - 1) // 2
    group = devices // chunks
    slot = lax.rem(c, 2)

    def proj_copy(step, where):
        return pltpu.make_async_copy(
            buf_ref.at[where].reshape(group, chunks, sub, width),
            out_hbm.at[pl.ds(step * group, group), pl.ds(0, chunks)],
            sem.at[where],
        )

    def other_copy(step, where):
        return pltpu.make_async_copy(buf_ref.at[where], out_hbm.at[:, step], sem.at[where])

    @pl.when(c >= 2)
    def _():
        other_copy(chunks, slot).wait()

    def put(value):
        buf_ref[slot] = value.astype(bf).reshape(devices, sub, width)

    @pl.when(c < chunks)
    def _():
        put(tn(act_ref[...], og_ref[...]))
        proj_copy(c, slot).start()

    @pl.when((c >= chunks) & (c < 2 * chunks))
    def _():
        put(tn(n2_ref[...], gp_ref[...]))
        other_copy(c, slot).start()

    @pl.when(c == last)
    def _():
        put(tn(mixed_ref[...], gml_ref[...]))
        other_copy(c, slot).start()
        other_copy(chunks, 1 - slot).wait()
        other_copy(chunks, slot).wait()


def weight_grads(act, gp, og, n2, mixed, gml, devices):
    rows, width = og.shape
    chunks = act.shape[1] // width
    slots = 2 * chunks + 1
    sub = width // devices
    fixed = pl.BlockSpec((rows, width), lambda c: (0, 0))
    return pl.pallas_call(
        weight_grad_kernel,
        grid=(slots,),
        in_specs=[
            pl.BlockSpec((rows, width), lambda c: (0, jnp.minimum(c, chunks - 1))),
            pl.BlockSpec((rows, width), lambda c: (0, jnp.clip(c - chunks, 0, chunks - 1))),
            fixed,
            fixed,
            fixed,
            fixed,
        ],
        out_specs=pl.BlockSpec(memory_space=pl.ANY),
        out_shape=jax.ShapeDtypeStruct((devices, slots, sub, width), bf),
        scratch_shapes=[
            pltpu.VMEM((2, devices, sub, width), bf),
            pltpu.SemaphoreType.DMA((2,)),
        ],
        cost_estimate=busy(19),
        name="weight_grads",
    )(act, gp, og, n2, mixed, gml)


def norm_sums_kernel(
    place_ref,
    own_ref,
    other_ref,
    g0_ref,
    g1_ref,
    g2_ref,
    r0_ref,
    r1_ref,
    w_ref,
    wo_ref,
    e_ref,
    sums_ref,
    bias_ref,
):
    i = pl.program_id(0)
    per_side = pl.num_programs(0) // 2
    is_own = i // per_side == place_ref[0]

    @pl.when(i == 0)
    def _():
        sums_ref[...] = jnp.zeros_like(sums_ref)
        bias_ref[...] = jnp.zeros_like(bias_ref)

    unit, _ = norm_stats(jnp.where(is_own, own_ref[...], other_ref[...]).astype(f32))
    wide = 3 * PAIR
    e = None
    for p, g_ref in enumerate((g0_ref, g1_ref, g2_ref)):
        cols = slice(p * wide, (p + 1) * wide)
        g = g_ref[...]
        part = nt(g, w_ref[:, cols])
        e = part if e is None else e + part
        bias_ref[0:1, cols] += jnp.sum(g.astype(f32), axis=0, keepdims=True)
    sums_ref[0:1, :] += jnp.sum(e * unit, axis=0, keepdims=True)
    sums_ref[1:2, :] += jnp.sum(e, axis=0, keepdims=True)

    @pl.when(is_own)
    def _():
        total = e
        for p, r_ref in enumerate((r0_ref, r1_ref)):
            total = total + nt(r_ref[...], wo_ref[:, p * wide : (p + 1) * wide])
        e_ref[...] = total


def norm_sums(place, own, other, grads, received, weight, weight_other, block=256):
    rows, width = own.shape
    per_side = rows // block
    cols = weight.shape[1]
    mine = lambda i, s: (jnp.clip(i - s[0] * per_side, 0, per_side - 1), 0)
    theirs = lambda i, s: (jnp.clip(i - (1 - s[0]) * per_side, 0, per_side - 1), 0)
    fixed = lambda shape: pl.BlockSpec(shape, lambda i, s: (0, 0))
    return pl.pallas_call(
        norm_sums_kernel,
        grid_spec=pltpu.PrefetchScalarGridSpec(
            num_scalar_prefetch=1,
            grid=(2 * per_side,),
            in_specs=[
                pl.BlockSpec((block, width), mine),
                pl.BlockSpec((block, width), theirs),
                *[pl.BlockSpec((block, 3 * PAIR), lambda i, s: (i, 0))] * 3,
                *[pl.BlockSpec((block, 3 * PAIR), mine)] * 2,
                fixed(weight.shape),
                fixed(weight.shape),
            ],
            out_specs=[pl.BlockSpec((block, width), mine), fixed((8, width)), fixed((8, cols))],
        ),
        out_shape=[
            jax.ShapeDtypeStruct((rows, width), f32),
            jax.ShapeDtypeStruct((8, width), f32),
            jax.ShapeDtypeStruct((8, cols), f32),
        ],
        cost_estimate=busy(13),
        name="norm_sums",
    )(place, own, other, *grads, *received, weight, weight_other)


def finish_kernel(x_ref, gm_ref, e_ref, r_ref, wo_ref, gain_ref, out_ref):
    unit, scale = norm_stats(x_ref[...].astype(f32))
    eg = (e_ref[...] + nt(r_ref[...], wo_ref[...])) * gain_ref[...]
    out_ref[...] = gm_ref[...] + scale * (
        eg
        - jnp.mean(eg, axis=-1, keepdims=True)
        - unit * jnp.mean(eg * unit, axis=-1, keepdims=True)
    )


def finish(x, grad_middle, e, received, weight_other, gain, block=256):
    rows, width = x.shape
    row = lambda cols: pl.BlockSpec((block, cols), lambda i: (i, 0))
    last = weight_other.shape[1] // (3 * PAIR) - 1
    return pl.pallas_call(
        finish_kernel,
        grid=(rows // block,),
        in_specs=[
            row(width),
            row(width),
            row(width),
            row(3 * PAIR),
            pl.BlockSpec((width, 3 * PAIR), lambda i: (0, last)),
            pl.BlockSpec((1, width), lambda i: (0, 0)),
        ],
        out_specs=row(width),
        out_shape=jax.ShapeDtypeStruct((rows, width), f32),
        cost_estimate=busy(6),
        name="finish",
    )(x, grad_middle, e, received, weight_other, gain)


AXES = ("dp", "fsdp")


def swap(value, bit, total):
    return lax.ppermute(value, AXES, [(i, i ^ bit) for i in range(total)])


def gather_dp(shard, dp_size, order):
    me = lax.axis_index("dp")
    bits = dp_size.bit_length() - 1
    held = shard.reshape((1,) * bits + shard.shape)
    for bit in order:
        other = swap(held, 2 << bit, 2 * dp_size)
        low = (me >> bit) & 1 == 0
        held = jnp.concatenate(
            [jnp.where(low, held, other), jnp.where(low, other, held)], axis=bits - 1 - bit
        )
    return held.reshape((dp_size * shard.shape[0],) + shard.shape[1:])


def scatter_dp(whole, dp_size, order):
    me = lax.axis_index("dp")
    bits = dp_size.bit_length() - 1
    rows = whole.shape[0] // dp_size
    held = whole.reshape((2,) * bits + (rows,) + whole.shape[1:])
    for bit in order:
        axis = bits - 1 - bit
        low = (me >> bit) & 1 == 0
        first = lax.slice_in_dim(held, 0, 1, axis=axis)
        second = lax.slice_in_dim(held, 1, 2, axis=axis)
        mine = jnp.where(low, first, second)
        sent = jnp.where(low, second, first).astype(bf)
        held = mine.astype(f32) + swap(sent, 2 << bit, 2 * dp_size).astype(
            f32
        )
    return held.reshape((rows,) + whole.shape[1:])


def sum_all(vector, total):
    bits = [1 << b for b in range(total.bit_length() - 1)]
    for bit in bits[1:] + bits[:1]:
        vector = vector + swap(vector, bit, total)
    return vector


def on_device_pair(
    dp_size,
    block_input,
    seq_long,
    ln1_gain,
    ln1_bias,
    w_qkv,
    b_qkv,
    w_out,
    b_out,
    ln2_gain,
    ln2_bias,
    w_fc,
    b_fc,
    w_proj,
    b_proj,
    out_grad,
):
    total = 2 * dp_size
    side = lax.axis_index("fsdp")
    flat = lax.axis_index("dp") * 2 + side
    on_left = side == 0
    row_total = block_input.shape[0]
    half = D // 2
    dp_bits = list(range(dp_size.bit_length() - 1))
    gather_order = dp_bits[1:2] + dp_bits[:1:-1] + dp_bits[:1]
    scatter_order = dp_bits[:1] + dp_bits[2:] + dp_bits[1:2]

    def ordered(mine, other, axis):
        return jnp.concatenate(
            [jnp.where(on_left, mine, other), jnp.where(on_left, other, mine)], axis=axis
        )

    pairs = half // PAIR

    def head_columns(rows_in, which):
        split = rows_in.reshape(rows_in.shape[0], 3, 2, pairs, PAIR)
        mine = lax.dynamic_index_in_dim(split, which, 2, keepdims=False)
        return jnp.transpose(mine, (0, 2, 1, 3)).reshape(rows_in.shape[0], 3 * half)

    def rows_of(whole, which):
        return lax.dynamic_slice_in_dim(whole, which * row_total, row_total, axis=0)

    small = (ln1_gain, ln1_bias, b_qkv, b_out, ln2_gain, ln2_bias, b_fc, b_proj)
    placed = jnp.concatenate(
        [
            lax.dynamic_update_slice(
                jnp.zeros((item.shape[0] * total,), bf), item, (item.shape[0] * flat,)
            )
            for item in small
        ]
    )
    gathered = sum_all(placed, total).astype(f32)
    pieces = []
    start = 0
    for item in small:
        pieces.append(gathered[start : start + item.shape[0] * total])
        start += item.shape[0] * total
    ln1_gain, ln1_bias, b_qkv, b_out, ln2_gain, ln2_bias, b_fc, b_proj = pieces

    other_input = swap(block_input, 1, total)
    received = swap(head_columns(w_qkv, 1 - side), 1, total)
    w_mine = gather_dp(ordered(head_columns(w_qkv, side), received, 0), dp_size, gather_order)
    w_other = swap(w_mine, 1, total)

    sub = w_out.shape[0]
    chunks = FF // D
    packed = jnp.concatenate(
        [w_proj] + [w_fc[:, c * D : (c + 1) * D] for c in range(chunks)] + [w_out], axis=0
    )
    gathered_w = lax.all_gather(packed, AXES, axis=0, tiled=True)
    gathered_w = gathered_w.reshape(total, 2 * chunks + 1, sub, D)

    def as_row(vector):
        return vector.reshape(1, -1)

    place = side.astype(jnp.int32).reshape(1)
    b_mine = head_columns(as_row(b_qkv), side)
    normed_one, projected = project(
        place, block_input, other_input, as_row(ln1_gain), as_row(ln1_bias), w_mine, b_mine
    )
    heads_mine = []
    heads_other = []
    log_totals = []
    for p in range(pairs):
        heads, log_total = attend_fwd(seq_long, projected, p)
        heads_mine.append(heads)
        log_totals.append(log_total)
        heads_other.append(swap(rows_of(heads, 1 - side), 1, total))
    (
        block_output,
        mixed,
        normed_two,
        hidden_act,
        grad_pre,
        grad_middle,
        grad_mid_low,
        *rest,
    ) = mlp(
        place,
        gathered_w,
        block_input,
        out_grad,
        heads_mine,
        heads_other,
        as_row(b_out),
        as_row(ln2_gain),
        as_row(ln2_bias),
        as_row(b_fc),
        as_row(b_proj),
    )
    grad_keep = rest[:pairs]
    grad_other = [swap(item, 1, total) for item in rest[pairs : 2 * pairs]]
    sums = rest[2 * pairs]
    packed_grads = weight_grads(
        hidden_act, grad_pre, out_grad, normed_two, mixed, grad_mid_low, total
    )
    shard = lax.psum_scatter(
        packed_grads.reshape(total * (2 * chunks + 1) * sub, D),
        AXES,
        scatter_dimension=0,
        tiled=True,
    ).astype(f32)
    shard_w_proj = shard[: chunks * sub]
    shard_w_fc = jnp.concatenate(
        [shard[(chunks + c) * sub : (chunks + c + 1) * sub] for c in range(chunks)], axis=1
    )
    shard_w_out = shard[2 * chunks * sub :]
    grad_b_fc = sums[0]
    grad_b_proj, grad_ln2_gain, grad_ln2_bias, grad_b_out = (
        sums[1, k * D : (k + 1) * D] for k in range(4)
    )
    grads = []
    grads_other = []
    shards = []
    for p in range(pairs):
        grad_pair = attend_bwd(
            seq_long,
            place,
            projected,
            p,
            heads_mine[p],
            grad_keep[p],
            grad_other[p],
            log_totals[p],
        )
        grads.append(grad_pair)
        grads_other.append(swap(rows_of(grad_pair, 1 - side), 1, total))
        shards.append(scatter_dp(product_tn(normed_one, grad_pair), dp_size, scatter_order))

    e_partial, norm_one_sums, grad_b_mine = norm_sums(
        place, block_input, other_input, grads, grads_other[:-1], w_mine, w_other
    )
    input_grad = finish(
        block_input, grad_middle, e_partial, grads_other[-1], w_other, as_row(ln1_gain)
    )

    shard_rows = jnp.concatenate(shards, axis=1).reshape(2, -1, 3 * half)
    keep = lax.dynamic_index_in_dim(shard_rows, side, 0, keepdims=False)
    send = lax.dynamic_index_in_dim(shard_rows, 1 - side, 0, keepdims=False)
    taken = swap(send, 1, total)

    def by_part(rows_in):
        split = rows_in.reshape(rows_in.shape[0], pairs, 3, PAIR)
        return jnp.transpose(split, (0, 2, 1, 3)).reshape(rows_in.shape[0], 3, 1, half)

    shard_w_qkv = ordered(by_part(keep), by_part(taken), 2).reshape(-1, 3 * D)
    grad_b_part = by_part(grad_b_mine[0:1])
    grad_b_qkv = ordered(grad_b_part, jnp.zeros_like(grad_b_part), 2).reshape(3 * D)
    grad_vectors = (
        grad_b_out,
        grad_ln2_gain,
        grad_ln2_bias,
        grad_b_fc,
        grad_b_proj,
        norm_one_sums[0],
        norm_one_sums[1],
        grad_b_qkv,
    )
    summed = sum_all(jnp.concatenate(grad_vectors), total)
    begin = 0
    vector_shards = []
    for item in grad_vectors:
        size = item.shape[0] // total
        vector_shards.append(lax.dynamic_slice(summed, (begin + size * flat,), (size,)))
        begin += item.shape[0]
    (
        shard_b_out,
        shard_ln2_gain,
        shard_ln2_bias,
        shard_b_fc,
        shard_b_proj,
        shard_ln1_gain,
        shard_ln1_bias,
        shard_b_qkv,
    ) = vector_shards
    return (
        block_output,
        input_grad,
        shard_ln1_gain,
        shard_ln1_bias,
        shard_w_qkv,
        shard_b_qkv,
        shard_w_out,
        shard_b_out,
        shard_ln2_gain,
        shard_ln2_bias,
        shard_w_fc,
        shard_b_fc,
        shard_w_proj,
        shard_b_proj,
    )


def solution(mesh):
    in_specs = (
        P(("dp", "fsdp"), None),
        P("dp"),
        P(("dp", "fsdp")),
        P(("dp", "fsdp")),
        P(("dp", "fsdp"), None),
        P(("dp", "fsdp")),
        P(("dp", "fsdp"), None),
        P(("dp", "fsdp")),
        P(("dp", "fsdp")),
        P(("dp", "fsdp")),
        P(("dp", "fsdp"), None),
        P(("dp", "fsdp")),
        P(("dp", "fsdp"), None),
        P(("dp", "fsdp")),
        P(("dp", "fsdp"), None),
    )
    out_specs = (
        P(("dp", "fsdp"), None),
        P(("dp", "fsdp"), None),
        P(("dp", "fsdp")),
        P(("dp", "fsdp")),
        P(("dp", "fsdp"), None),
        P(("dp", "fsdp")),
        P(("dp", "fsdp"), None),
        P(("dp", "fsdp")),
        P(("dp", "fsdp")),
        P(("dp", "fsdp")),
        P(("dp", "fsdp"), None),
        P(("dp", "fsdp")),
        P(("dp", "fsdp"), None),
        P(("dp", "fsdp")),
    )
    whole_slice = dict(mesh=mesh, in_specs=in_specs, out_specs=out_specs, check_vma=False)
    dp_size = mesh.shape["dp"]
    if mesh.shape["fsdp"] != 2 or dp_size < 8 or dp_size & (dp_size - 1):
        return jax.shard_map(on_device_generic, **whole_slice)

    def on_device(*args):
        return on_device_pair(dp_size, *args)

    return jax.shard_map(on_device, **whole_slice)
```

profile of v0, /device:TPU:0, one launch (start us, length us, event | category | flops | bytes accessed | tf_op | source)
XLA Modules:
  0.0 473.3 jit_solution(16370799340373485446)
XLA Ops:
  27.2 14.9 %collective-permute-done.8 = bf16[1,1,2,1,48,1152]{5,4,3,2,1,0:T(8,128)(2,1)S(1)} collective-permute-done((bf16[1,1,2,1,48,1152]{5,4,3,2,1,0:T(8,128)(2,1)S(1)}, bf16[1,1,2,1,48,1152]{5,4,3,2,1,0:T(8,128)(2,1)S(1)}, u32[]{:S(2)}, u32[]{:S(2)}) %collective-permute-start.8) | collective-permute-done | bytes 221216 | tf_op jit(solution)/shard_map/ppermute | solution.py:1052
  52.7 7.6 %collective-permute-done.3 = bf16[9984]{0:T(1024)(128)(2,1)S(1)} collective-permute-done((bf16[9984]{0:T(1024)(128)(2,1)S(1)}, bf16[9984]{0:T(1024)(128)(2,1)S(1)}, u32[]{:S(2)}, u32[]{:S(2)}) %collective-permute-start.3) | collective-permute-done | bytes 20000 | tf_op jit(solution)/shard_map/ppermute | solution.py:1052
  60.3 7.5 %collective-permute-start.4 = (bf16[9984]{0:T(1024)(128)(2,1)S(1)}, bf16[9984]{0:T(1024)(128)(2,1)S(1)}, u32[]{:S(2)}, u32[]{:S(2)}) collective-permute-start(bf16[9984]{0:T(1024)(128)(2,1)S(1)} %add.154), channel_id=1, source_target_pairs={{0,16},{1,17},{2,18},{3,19},{4,20},{5,21},{6,22},{7,23},{8,24},{9,... | collective-permute-start | bytes 59912 | tf_op jit(solution)/shard_map/ppermute | solution.py:1052
  71.7 45.2 %collective-permute-done.5 = bf16[9984]{0:T(1024)(128)(2,1)S(1)} collective-permute-done((bf16[9984]{0:T(1024)(128)(2,1)S(1)}, bf16[9984]{0:T(1024)(128)(2,1)S(1)}, u32[]{:S(2)}, u32[]{:S(2)}) %collective-permute-start.5) | collective-permute-done | bytes 20000 | tf_op jit(solution)/shard_map/ppermute | solution.py:1052
  120.3 11.6 %norm_project.1 = (bf16[2048,768]{1,0:T(8,128)(2,1)}, bf16[2048,1152]{1,0:T(8,128)(2,1)}) custom-call(s32[1]{0:T(128)} %bitcast.place_ref, bf16[1024,768]{1,0:T(8,128)(2,1)} %x_ref.3, bf16[1024,768]{1,0:T(8,128)(2,1)} %collective-permute-done.other_ref, f32[1,768]{1,0:T(1,128)} %reshape.196.gain_ref, f32[1,768]{1,0:T(1,128)} %reshape.197.bias_ref, ...), custom_call_target="tpu_custom_call" | custom-call | flops 12650000384 | bytes 11000000 | tf_op jit(solution)/shard_map/norm_project/pallas_call | solution.py:655
  131.9 10.0 %attend_fwd.4 = (bf16[2048,128]{1,0:T(8,128)(2,1)}, f32[8,2048]{1,0:T(8,128)}) custom-call(s32[1]{0:T(128)S(6)} %copy.79.flag_ref, bf16[2048,1152]{1,0:T(8,128)(2,1)} %get-tuple-element.39.q_ref.k_ref.v_ref, bf16[2048,1152]{1,0:T(8,128)(2,1)} %get-tuple-element.39.q_ref.k_ref.v_ref, bf16[2048,1152]{1,0:T(8,128)(2,1)} %get-tuple-element.39.q_ref.k_ref.v_ref), custom_call_target="tpu_custom_call" | custom-call | flops 18400000000 | bytes 16000000 | tf_op jit(solution)/shard_map/attend_fwd/pallas_call | solution.py:477
  144.6 10.2 %attend_fwd.5 = (bf16[2048,128]{1,0:T(8,128)(2,1)}, f32[8,2048]{1,0:T(8,128)}) custom-call(s32[1]{0:T(128)S(6)} %copy.79.flag_ref, bf16[2048,1152]{1,0:T(8,128)(2,1)} %get-tuple-element.39.q_ref.k_ref.v_ref, bf16[2048,1152]{1,0:T(8,128)(2,1)} %get-tuple-element.39.q_ref.k_ref.v_ref, bf16[2048,1152]{1,0:T(8,128)(2,1)} %get-tuple-element.39.q_ref.k_ref.v_ref), custom_call_target="tpu_custom_call" | custom-call | flops 18400000000 | bytes 16000000 | tf_op jit(solution)/shard_map/attend_fwd/pallas_call | solution.py:477
  156.2 9.9 %attend_fwd.3 = (bf16[2048,128]{1,0:T(8,128)(2,1)}, f32[8,2048]{1,0:T(8,128)}) custom-call(s32[1]{0:T(128)S(6)} %copy.79.flag_ref, bf16[2048,1152]{1,0:T(8,128)(2,1)} %get-tuple-element.39.q_ref.k_ref.v_ref, bf16[2048,1152]{1,0:T(8,128)(2,1)} %get-tuple-element.39.q_ref.k_ref.v_ref, bf16[2048,1152]{1,0:T(8,128)(2,1)} %get-tuple-element.39.q_ref.k_ref.v_ref), custom_call_target="tpu_custom_call" | custom-call | flops 18400000000 | bytes 16000000 | tf_op jit(solution)/shard_map/attend_fwd/pallas_call | solution.py:477
  172.1 4.2 collective-permute-done.11.hb0_ref
  177.0 37.6 %mlp.1 = (bf16[1024,768]{1,0:T(8,128)(2,1)}, bf16[1024,768]{1,0:T(8,128)(2,1)}, bf16[1024,768]{1,0:T(8,128)(2,1)}, bf16[1024,3072]{1,0:T(8,128)(2,1)}, bf16[1024...) custom-call(s32[1]{0:T(128)} %bitcast.place_ref, ...), custom_call_target="tpu_custom_call" | custom-call | flops 42550001664 | bytes 37000000 | tf_op jit(solution)/shard_map/mlp/pallas_call | solution.py:819
  214.6 19.2 %weight_grads.1 = bf16[32,9,24,768]{3,2,1,0:T(8,128)(2,1)} custom-call(bf16[1024,3072]{1,0:T(8,128)(2,1)} %get-tuple-element.59.act_ref, bf16[1024,3072]{1,0:T(8,128)(2,1)} %get-tuple-element.60.gp_ref, bf16[1024,768]{1,0:T(8,128)(2,1)} %og_ref.3, bf16[1024,768]{1,0:T(8,128)(2,1)} %get-tuple-element.61.n2_ref, ...), custom_call_target="tpu_custom_call" | custom-call | flops 21849999360 | bytes 19000000 | tf_op jit(solution)/shard_map/weight_grads/pallas_call | solution.py:918
  241.8 16.7 %attend_bwd.3.g0_ref = bf16[2048,384]{1,0:T(8,128)(2,1)} custom-call(s32[1]{0:T(128)S(6)} %copy.79.flag_ref, s32[1]{0:T(128)} %bitcast.place_ref, bf16[2048,1152]{1,0:T(8,128)(2,1)} %get-tuple-element.39.q_ref.k_ref.v_ref, bf16[2048,1152]{1,0:T(8,128)(2,1)} %get-tuple-element.39.q_ref.k_ref.v_ref, bf16[2048,1152]{1,0:T(8,128)(2,1)} %get-tuple-element.39.q_ref.k_ref.v_ref, ...), custom_call_target="tpu_custom_call" | custom-call | flops 28750000128 | bytes 25000000 | tf_op jit(solution)/shard_map/attend_bwd/pallas_call | solution.py:597
  263.6 16.9 %attend_bwd.4.g1_ref = bf16[2048,384]{1,0:T(8,128)(2,1)} custom-call(s32[1]{0:T(128)S(6)} %copy.79.flag_ref, s32[1]{0:T(128)} %bitcast.place_ref, bf16[2048,1152]{1,0:T(8,128)(2,1)} %get-tuple-element.39.q_ref.k_ref.v_ref, bf16[2048,1152]{1,0:T(8,128)(2,1)} %get-tuple-element.39.q_ref.k_ref.v_ref, bf16[2048,1152]{1,0:T(8,128)(2,1)} %get-tuple-element.39.q_ref.k_ref.v_ref, ...), custom_call_target="tpu_custom_call" | custom-call | flops 28750000128 | bytes 25000000 | tf_op jit(solution)/shard_map/attend_bwd/pallas_call | solution.py:597
  286.1 16.8 %attend_bwd.5.g2_ref = bf16[2048,384]{1,0:T(8,128)(2,1)} custom-call(s32[1]{0:T(128)S(6)} %copy.79.flag_ref, s32[1]{0:T(128)} %bitcast.place_ref, bf16[2048,1152]{1,0:T(8,128)(2,1)} %get-tuple-element.39.q_ref.k_ref.v_ref, bf16[2048,1152]{1,0:T(8,128)(2,1)} %get-tuple-element.39.q_ref.k_ref.v_ref, bf16[2048,1152]{1,0:T(8,128)(2,1)} %get-tuple-element.39.q_ref.k_ref.v_ref, ...), custom_call_target="tpu_custom_call" | custom-call | flops 28750000128 | bytes 25000000 | tf_op jit(solution)/shard_map/attend_bwd/pallas_call | solution.py:597
  313.4 47.1 %collective-permute-start.27 = (bf16[2,1,2,1,48,384]{5,4,3,2,1,0:T(8,128)(2,1)S(1)}, bf16[2,1,2,1,48,384]{5,4,3,2,1,0:T(8,128)(2,1)S(1)}, u32[]{:S(2)}, u32[]{:S(2)}) collective-permute-start(bf16[2,1,2,1,48,384]{5,4,3,2,1,0:T(8,128)(2,1)S(1)} %select_convert_fusion.5), channel_id=1, source_target_pairs={{0,8},{1,9},{2,10},{3,11},{4,12},{5,13},{6,14},{7,15},{8,0},{9,1},... | collective-permute-start | bytes 442376 | tf_op jit(solution)/shard_map/ppermute | solution.py:1052
  360.6 5.2 %collective-permute-done.27 = bf16[2,1,2,1,48,384]{5,4,3,2,1,0:T(8,128)(2,1)S(1)} collective-permute-done((bf16[2,1,2,1,48,384]{5,4,3,2,1,0:T(8,128)(2,1)S(1)}, bf16[2,1,2,1,48,384]{5,4,3,2,1,0:T(8,128)(2,1)S(1)}, u32[]{:S(2)}, u32[]{:S(2)}) %collective-permute-start.27) | collective-permute-done | bytes 147488 | tf_op jit(solution)/shard_map/ppermute | solution.py:1052
  368.3 6.5 %collective-permute-done.31 = bf16[2,1,2,1,48,384]{5,4,3,2,1,0:T(8,128)(2,1)S(1)} collective-permute-done((bf16[2,1,2,1,48,384]{5,4,3,2,1,0:T(8,128)(2,1)S(1)}, bf16[2,1,2,1,48,384]{5,4,3,2,1,0:T(8,128)(2,1)S(1)}, u32[]{:S(2)}, u32[]{:S(2)}) %collective-permute-start.31) | collective-permute-done | bytes 147488 | tf_op jit(solution)/shard_map/ppermute | solution.py:1052
  376.8 8.7 %collective-permute-done.35 = bf16[2,1,2,1,48,384]{5,4,3,2,1,0:T(8,128)(2,1)S(1)} collective-permute-done((bf16[2,1,2,1,48,384]{5,4,3,2,1,0:T(8,128)(2,1)S(1)}, bf16[2,1,2,1,48,384]{5,4,3,2,1,0:T(8,128)(2,1)S(1)}, u32[]{:S(2)}, u32[]{:S(2)}) %collective-permute-start.35) | collective-permute-done | bytes 147488 | tf_op jit(solution)/shard_map/ppermute | solution.py:1052
  386.2 5.6 %collective-permute-done.28 = bf16[1,1,2,1,48,384]{5,4,3,2,1,0:T(8,128)(2,1)S(1)} collective-permute-done((bf16[1,1,2,1,48,384]{5,4,3,2,1,0:T(8,128)(2,1)S(1)}, bf16[1,1,2,1,48,384]{5,4,3,2,1,0:T(8,128)(2,1)S(1)}, u32[]{:S(2)}, u32[]{:S(2)}) %collective-permute-start.28) | collective-permute-done | bytes 73760 | tf_op jit(solution)/shard_map/ppermute | solution.py:1052
  391.9 7.3 %collective-permute-done.32 = bf16[1,1,2,1,48,384]{5,4,3,2,1,0:T(8,128)(2,1)S(1)} collective-permute-done((bf16[1,1,2,1,48,384]{5,4,3,2,1,0:T(8,128)(2,1)S(1)}, bf16[1,1,2,1,48,384]{5,4,3,2,1,0:T(8,128)(2,1)S(1)}, u32[]{:S(2)}, u32[]{:S(2)}) %collective-permute-start.32) | collective-permute-done | bytes 73760 | tf_op jit(solution)/shard_map/ppermute | solution.py:1052
  399.3 8.5 %collective-permute-done.36 = bf16[1,1,2,1,48,384]{5,4,3,2,1,0:T(8,128)(2,1)S(1)} collective-permute-done((bf16[1,1,2,1,48,384]{5,4,3,2,1,0:T(8,128)(2,1)S(1)}, bf16[1,1,2,1,48,384]{5,4,3,2,1,0:T(8,128)(2,1)S(1)}, u32[]{:S(2)}, u32[]{:S(2)}) %collective-permute-start.36) | collective-permute-done | bytes 73760 | tf_op jit(solution)/shard_map/ppermute | solution.py:1052
  421.7 13.9 %norm_sums.1 = (f32[1024,768]{1,0:T(8,128)}, f32[8,768]{1,0:T(8,128)}, f32[8,1152]{1,0:T(8,128)}) custom-call(s32[1]{0:T(128)} %bitcast.place_ref, bf16[1024,768]{1,0:T(8,128)(2,1)} %x_ref.3, bf16[1024,768]{1,0:T(8,128)(2,1)} %collective-permute-done.other_ref, bf16[2048,384]{1,0:T(8,128)(2,1)} %attend_bwd.3.g0_ref, bf16[2048,384]{1,0:T(8,128)(2,1)} %attend_bwd.4.g1_ref, ...), custom_call_target="tpu_custom_call" | custom-call | flops 14949999616 | bytes 13000000 | tf_op jit(solution)/shard_map/norm_sums/pallas_call | solution.py:991
  443.1 3.7 collective-permute-done.23
  453.6 7.0 %finish.1 = f32[1024,768]{1,0:T(8,128)} custom-call(bf16[1024,768]{1,0:T(8,128)(2,1)} %x_ref.3, f32[1024,768]{1,0:T(8,128)} %get-tuple-element.44.gm_ref, f32[1024,768]{1,0:T(8,128)} %get-tuple-element.54.e_ref, bf16[1024,384]{1,0:T(8,128)(2,1)} %copy-done.9, bf16[768,1152]{1,0:T(8,128)(2,1)} %collective-permute-done.19.wo_ref, f32[1,768]{1,0:T(1,128)} %reshape.196.gain_ref), custom_call_target="tpu_custom_call" | custom-call | flops 6899999744 | bytes 6000000 | tf_op jit(solution)/shard_map/finish/pallas_call | solution.py:1030
  (264 shorter events, 116.1 us)
Async XLA Ops:
  7.2 169.1 %all-gather.2.cloned.1.call-start = ((), (), s32[]{:S(2)}) async-start(), calls=%async_computation.1 | async-start | bytes 10948608 | tf_op jit(solution)/shard_map/all_gather | solution.py:1163
  12.8 449.7 %reduce-scatter.2.cloned.1.call-start = ((), (), s32[]{:S(2)}) async-start(), calls=%async_computation.2 | async-start | bytes 10948608 | tf_op jit(solution)/shard_map/reduce_scatter | solution.py:1210
  24.1 18.0 %collective-permute-start.8 = (bf16[1,1,2,1,48,1152]{5,4,3,2,1,0:T(8,128)(2,1)S(1)}, bf16[1,1,2,1,48,1152]{5,4,3,2,1,0:T(8,128)(2,1)S(1)}, u32[]{:S(2)}, u32[]{:S(2)}) collective-permute-start(bf16[1,1,2,1,48,1152]{5,4,3,2,1,0:T(8,128)(2,1)S(1)} %pad_maximum_fusion.4), channel_id=1, source_target_pairs={{0,16},{1,17},{2,18},{3,19},{4,20},{5,21},{6,22},{7,23},{8,24},{9,... | collective-permute-start | bytes 663560 | tf_op jit(solution)/shard_map/ppermute | solution.py:1052
  42.2 29.2 %collective-permute-start.9 = (bf16[2,1,2,1,48,1152]{5,4,3,2,1,0:T(8,128)(2,1)S(1)}, bf16[2,1,2,1,48,1152]{5,4,3,2,1,0:T(8,128)(2,1)S(1)}, u32[]{:S(2)}, u32[]{:S(2)}) collective-permute-start(bf16[2,1,2,1,48,1152]{5,4,3,2,1,0:T(8,128)(2,1)S(1)} %pad_maximum_fusion.2), channel_id=1, source_target_pairs={{0,8},{1,9},{2,10},{3,11},{4,12},{5,13},{6,14},{7,15},{8,0},{9,1},... | collective-permute-start | bytes 1327112 | tf_op jit(solution)/shard_map/ppermute | solution.py:1052
  60.3 9.7 %collective-permute-start.4 = (bf16[9984]{0:T(1024)(128)(2,1)S(1)}, bf16[9984]{0:T(1024)(128)(2,1)S(1)}, u32[]{:S(2)}, u32[]{:S(2)}) collective-permute-start(bf16[9984]{0:T(1024)(128)(2,1)S(1)} %add.154), channel_id=1, source_target_pairs={{0,16},{1,17},{2,18},{3,19},{4,20},{5,21},{6,22},{7,23},{8,24},{9,... | collective-permute-start | bytes 59912 | tf_op jit(solution)/shard_map/ppermute | solution.py:1052
  67.8 52.4 %collective-permute-start = (bf16[1024,768]{1,0:T(8,128)(2,1)}, bf16[1024,768]{1,0:T(8,128)(2,1)}, u32[]{:S(2)}, u32[]{:S(2)}) collective-permute-start(bf16[1024,768]{1,0:T(8,128)(2,1)} %x_ref.3), channel_id=1, source_target_pairs={{0,1},{1,0},{2,3},{3,2},{4,5},{5,4},{6,7},{7,6},{8,9},{9,8},{10,11... | collective-permute-start | bytes 4718600 | tf_op jit(solution)/shard_map/ppermute | solution.py:1052
  70.1 46.7 %collective-permute-start.5 = (bf16[9984]{0:T(1024)(128)(2,1)S(1)}, bf16[9984]{0:T(1024)(128)(2,1)S(1)}, u32[]{:S(2)}, u32[]{:S(2)}) collective-permute-start(bf16[9984]{0:T(1024)(128)(2,1)S(1)} %add.155), channel_id=1, source_target_pairs={{0,1},{1,0},{2,3},{3,2},{4,5},{5,4},{6,7},{7,6},{8,9},{9,8},{10,11... | collective-permute-start | bytes 59912 | tf_op jit(solution)/shard_map/ppermute | solution.py:1052
  71.6 47.1 %collective-permute-start.10 = (bf16[2,2,2,1,48,1152]{5,4,3,2,1,0:T(8,128)(2,1)S(1)}, bf16[2,2,2,1,48,1152]{5,4,3,2,1,0:T(8,128)(2,1)S(1)}, u32[]{:S(2)}, u32[]{:S(2)}) collective-permute-start(bf16[2,2,2,1,48,1152]{5,4,3,2,1,0:T(8,128)(2,1)S(1)} %pad_maximum_fusion.1), channel_id=1, source_target_pairs={{0,2},{1,3},{2,0},{3,1},{4,6},{5,7},{6,4},{7,5},{8,10},{9,11},{10,... | collective-permute-start | bytes 2654216 | tf_op jit(solution)/shard_map/ppermute | solution.py:1052
  142.9 29.2 %collective-permute-start.12 = (bf16[1024,128]{1,0:T(8,128)(2,1)S(1)}, bf16[1024,128]{1,0:T(8,128)(2,1)S(1)}, u32[]{:S(2)}, u32[]{:S(2)}) collective-permute-start(bf16[1024,128]{1,0:T(8,128)(2,1)S(1)} %constant_dynamic-slice_fusion.5), channel_id=1, source_target_pairs={{0,1},{1,0},{2,3},{3,2},{4,5},{5,4},{6,7},{7,6},{8,9},{9,8},{10,11... | collective-permute-start | bytes 786440 | tf_op jit(solution)/shard_map/ppermute | solution.py:1052
  155.8 16.2 %collective-permute-start.13 = (bf16[1024,128]{1,0:T(8,128)(2,1)S(1)}, bf16[1024,128]{1,0:T(8,128)(2,1)S(1)}, u32[]{:S(2)}, u32[]{:S(2)}) collective-permute-start(bf16[1024,128]{1,0:T(8,128)(2,1)S(1)} %constant_dynamic-slice_fusion.4), channel_id=1, source_target_pairs={{0,1},{1,0},{2,3},{3,2},{4,5},{5,4},{6,7},{7,6},{8,9},{9,8},{10,11... | collective-permute-start | bytes 786440 | tf_op jit(solution)/shard_map/ppermute | solution.py:1052
  167.0 9.2 %collective-permute-start.11 = (bf16[1024,128]{1,0:T(8,128)(2,1)S(1)}, bf16[1024,128]{1,0:T(8,128)(2,1)S(1)}, u32[]{:S(2)}, u32[]{:S(2)}) collective-permute-start(bf16[1024,128]{1,0:T(8,128)(2,1)S(1)} %constant_dynamic-slice_fusion.6), channel_id=1, source_target_pairs={{0,1},{1,0},{2,3},{3,2},{4,5},{5,4},{6,7},{7,6},{8,9},{9,8},{10,11... | collective-permute-start | bytes 786440 | tf_op jit(solution)/shard_map/ppermute | solution.py:1052
  171.7 249.1 %collective-permute-start.19 = (bf16[768,1152]{1,0:T(8,128)(2,1)}, bf16[768,1152]{1,0:T(8,128)(2,1)}, u32[]{:S(2)}, u32[]{:S(2)}) collective-permute-start(bf16[768,1152]{1,0:T(8,128)(2,1)} %bitcast.7.w_ref), channel_id=1, source_target_pairs={{0,1},{1,0},{2,3},{3,2},{4,5},{5,4},{6,7},{7,6},{8,9},{9,8},{10,11... | collective-permute-start | bytes 5308424 | tf_op jit(solution)/shard_map/ppermute | solution.py:1052
  236.4 27.1 %collective-permute-start.15 = (bf16[1024,128]{1,0:T(8,128)(2,1)}, bf16[1024,128]{1,0:T(8,128)(2,1)}, u32[]{:S(2)}, u32[]{:S(2)}) collective-permute-start(bf16[1024,128]{1,0:T(8,128)(2,1)} %get-tuple-element.49), channel_id=1, source_target_pairs={{0,1},{1,0},{2,3},{3,2},{4,5},{5,4},{6,7},{7,6},{8,9},{9,8},{10,11... | collective-permute-start | bytes 786440 | tf_op jit(solution)/shard_map/ppermute | solution.py:1052
  236.8 49.3 %collective-permute-start.16 = (bf16[1024,128]{1,0:T(8,128)(2,1)}, bf16[1024,128]{1,0:T(8,128)(2,1)}, u32[]{:S(2)}, u32[]{:S(2)}) collective-permute-start(bf16[1024,128]{1,0:T(8,128)(2,1)} %get-tuple-element.52), channel_id=1, source_target_pairs={{0,1},{1,0},{2,3},{3,2},{4,5},{5,4},{6,7},{7,6},{8,9},{9,8},{10,11... | collective-permute-start | bytes 786440 | tf_op jit(solution)/shard_map/ppermute | solution.py:1052
  263.6 46.5 %collective-permute-start.26 = (bf16[2,2,2,1,48,384]{5,4,3,2,1,0:T(8,128)(2,1)}, bf16[2,2,2,1,48,384]{5,4,3,2,1,0:T(8,128)(2,1)S(1)}, u32[]{:S(2)}, u32[]{:S(2)}) collective-permute-start(bf16[2,2,2,1,48,384]{5,4,3,2,1,0:T(8,128)(2,1)} %select_convert_fusion.2), channel_id=1, source_target_pairs={{0,2},{1,3},{2,0},{3,1},{4,6},{5,7},{6,4},{7,5},{8,10},{9,11},{10,... | collective-permute-start | bytes 884744 | tf_op jit(solution)/shard_map/ppermute | solution.py:1052
  285.6 24.9 %collective-permute-start.30 = (bf16[2,2,2,1,48,384]{5,4,3,2,1,0:T(8,128)(2,1)}, bf16[2,2,2,1,48,384]{5,4,3,2,1,0:T(8,128)(2,1)}, u32[]{:S(2)}, u32[]{:S(2)}) collective-permute-start(bf16[2,2,2,1,48,384]{5,4,3,2,1,0:T(8,128)(2,1)} %select_convert_fusion.1), channel_id=1, source_target_pairs={{0,2},{1,3},{2,0},{3,1},{4,6},{5,7},{6,4},{7,5},{8,10},{9,11},{10,... | collective-permute-start | bytes 884744 | tf_op jit(solution)/shard_map/ppermute | solution.py:1052
  308.4 112.4 %collective-permute-start.18 = (bf16[1024,384]{1,0:T(8,128)(2,1)S(1)}, bf16[1024,384]{1,0:T(8,128)(2,1)S(1)}, u32[]{:S(2)}, u32[]{:S(2)}) collective-permute-start(bf16[1024,384]{1,0:T(8,128)(2,1)S(1)} %constant_dynamic-slice_fusion.2), channel_id=1, source_target_pairs={{0,1},{1,0},{2,3},{3,2},{4,5},{5,4},{6,7},{7,6},{8,9},{9,8},{10,11... | collective-permute-start | bytes 2359304 | tf_op jit(solution)/shard_map/ppermute | solution.py:1052
  310.1 111.6 %collective-permute-start.17 = (bf16[1024,384]{1,0:T(8,128)(2,1)S(1)}, bf16[1024,384]{1,0:T(8,128)(2,1)}, u32[]{:S(2)}, u32[]{:S(2)}) collective-permute-start(bf16[1024,384]{1,0:T(8,128)(2,1)S(1)} %constant_dynamic-slice_fusion.3), channel_id=1, source_target_pairs={{0,1},{1,0},{2,3},{3,2},{4,5},{5,4},{6,7},{7,6},{8,9},{9,8},{10,11... | collective-permute-start | bytes 2359304 | tf_op jit(solution)/shard_map/ppermute | solution.py:1052
  310.5 142.2 %collective-permute-start.20 = (bf16[1024,384]{1,0:T(8,128)(2,1)S(1)}, bf16[1024,384]{1,0:T(8,128)(2,1)S(1)}, u32[]{:S(2)}, u32[]{:S(2)}) collective-permute-start(bf16[1024,384]{1,0:T(8,128)(2,1)S(1)} %constant_dynamic-slice_fusion.1), channel_id=1, source_target_pairs={{0,1},{1,0},{2,3},{3,2},{4,5},{5,4},{6,7},{7,6},{8,9},{9,8},{10,11... | collective-permute-start | bytes 2359304 | tf_op jit(solution)/shard_map/ppermute | solution.py:1052
  313.4 52.4 %collective-permute-start.27 = (bf16[2,1,2,1,48,384]{5,4,3,2,1,0:T(8,128)(2,1)S(1)}, bf16[2,1,2,1,48,384]{5,4,3,2,1,0:T(8,128)(2,1)S(1)}, u32[]{:S(2)}, u32[]{:S(2)}) collective-permute-start(bf16[2,1,2,1,48,384]{5,4,3,2,1,0:T(8,128)(2,1)S(1)} %select_convert_fusion.5), channel_id=1, source_target_pairs={{0,8},{1,9},{2,10},{3,11},{4,12},{5,13},{6,14},{7,15},{8,0},{9,1},... | collective-permute-start | bytes 442376 | tf_op jit(solution)/shard_map/ppermute | solution.py:1052
  365.8 9.0 %collective-permute-start.31 = (bf16[2,1,2,1,48,384]{5,4,3,2,1,0:T(8,128)(2,1)S(1)}, bf16[2,1,2,1,48,384]{5,4,3,2,1,0:T(8,128)(2,1)S(1)}, u32[]{:S(2)}, u32[]{:S(2)}) collective-permute-start(bf16[2,1,2,1,48,384]{5,4,3,2,1,0:T(8,128)(2,1)S(1)} %select_convert_fusion.4), channel_id=1, source_target_pairs={{0,8},{1,9},{2,10},{3,11},{4,12},{5,13},{6,14},{7,15},{8,0},{9,1},... | collective-permute-start | bytes 442376 | tf_op jit(solution)/shard_map/ppermute | solution.py:1052
  374.8 10.6 %collective-permute-start.35 = (bf16[2,1,2,1,48,384]{5,4,3,2,1,0:T(8,128)(2,1)S(1)}, bf16[2,1,2,1,48,384]{5,4,3,2,1,0:T(8,128)(2,1)S(1)}, u32[]{:S(2)}, u32[]{:S(2)}) collective-permute-start(bf16[2,1,2,1,48,384]{5,4,3,2,1,0:T(8,128)(2,1)S(1)} %select_convert_fusion.3), channel_id=1, source_target_pairs={{0,8},{1,9},{2,10},{3,11},{4,12},{5,13},{6,14},{7,15},{8,0},{9,1},... | collective-permute-start | bytes 442376 | tf_op jit(solution)/shard_map/ppermute | solution.py:1052
  419.8 20.7 %collective-permute-start.38 = (f32[24,1152]{1,0:T(8,128)S(1)}, f32[24,1152]{1,0:T(8,128)S(1)}, u32[]{:S(2)}, u32[]{:S(2)}) collective-permute-start(f32[24,1152]{1,0:T(8,128)S(1)} %get-tuple-element.86), channel_id=1, source_target_pairs={{0,1},{1,0},{2,3},{3,2},{4,5},{5,4},{6,7},{7,6},{8,9},{9,8},{10,11... | collective-permute-start | bytes 331784 | tf_op jit(solution)/shard_map/ppermute | solution.py:1052
  451.7 8.9 %collective-permute-start.25 = (f32[9984]{0:T(1024)S(1)}, f32[9984]{0:T(1024)S(1)}, u32[]{:S(2)}, u32[]{:S(2)}) collective-permute-start(f32[9984]{0:T(1024)S(1)} %add.163), channel_id=1, source_target_pairs={{0,1},{1,0},{2,3},{3,2},{4,5},{5,4},{6,7},{7,6},{8,9},{9,8},{10,11... | collective-permute-start | bytes 119816 | tf_op jit(solution)/shard_map/ppermute | solution.py:1052
  (41 other events, 345.8 us)
Sparse Core Ops, SparseCore 0:
  12.9 114.2 all-gather.1
  234.0 175.0 reduce-scatter.1
where the time goes:
time: 480 us; the launch traced here: 473 us
  Pallas kernels  170 us (35%)
  waiting for transfers between devices  140 us (29%)
  starting transfers between devices  96.3 us (20%)
  local copies, waits for them, and re-layouts  34.6 us (7%)
  between operations  15.7 us (3%)
  matrix products  9.89 us (2%)
  other arithmetic  6.92 us (1%)
    ppermute x39, waiting for transfers between devices, swap(): return lax.ppermute(value, AXES, [(i, i ^ bit) for i in range(total)])  140 us
    ppermute x39, starting transfers between devices, swap(): return lax.ppermute(value, AXES, [(i, i ^ bit) for i in range(total)])  96.2 us
    pallas_call x3, Pallas kernels, attend_bwd(): pl.pallas_call(functools.partial(attend_bwd_kernel, block, strips), grid_...  50.3 us
    pallas_call x1, Pallas kernels, mlp(): pl.pallas_call(mlp_kernel, grid_spec=pltpu.PrefetchScalarGridSpec(num_sca...  37.6 us
    pallas_call x3, Pallas kernels, attend_fwd(): pl.pallas_call(functools.partial(attend_fwd_kernel, block, strips), grid_...  30.1 us
    pallas_call x1, Pallas kernels, weight_grads(): pl.pallas_call(weight_grad_kernel, grid=(slots,), in_specs=[pl.BlockSpec(...  19.2 us
    unnamed x67, local copies, waits for them, and re-layouts  14 us
    pallas_call x1, Pallas kernels, norm_sums(): pl.pallas_call(norm_sums_kernel, grid_spec=pltpu.PrefetchScalarGridSpec(n...  13.9 us
  transfers between devices with their start and end apart: 41, of which 22 were waited for; matrix products, arithmetic and copies ran while one was open for 7% of the time, Pallas kernels for 36%

commit v1 on v0

--- a/solution.py
+++ b/solution.py
@@ -12,7 +12,6 @@
 f32 = jnp.float32
 bf = jnp.bfloat16
 
-
 D = 768
 HEADS = 12
 HD = 64
@@ -22,6 +21,7 @@
 
 EPS = 1e-05
 FAR = -1e30
+AXES = ("dp", "fsdp")
 
 
 def layer_norm(rows_in, gain_vec, bias_vec):
@@ -330,50 +330,50 @@
     long_flag = seq_long[0]
     fsdp_index = lax.axis_index("fsdp")
     weight_set = (
-        lax.all_gather(ln1_gain, ("dp", "fsdp"), axis=0, tiled=True),
-        lax.all_gather(ln1_bias, ("dp", "fsdp"), axis=0, tiled=True),
-        lax.all_gather(w_qkv, ("dp", "fsdp"), axis=0, tiled=True),
-        lax.all_gather(b_qkv, ("dp", "fsdp"), axis=0, tiled=True),
-        lax.all_gather(w_out, ("dp", "fsdp"), axis=0, tiled=True),
-        lax.all_gather(b_out, ("dp", "fsdp"), axis=0, tiled=True),
-        lax.all_gather(ln2_gain, ("dp", "fsdp"), axis=0, tiled=True),
-        lax.all_gather(ln2_bias, ("dp", "fsdp"), axis=0, tiled=True),
-        lax.all_gather(w_fc, ("dp", "fsdp"), axis=0, tiled=True),
-        lax.all_gather(b_fc, ("dp", "fsdp"), axis=0, tiled=True),
-        lax.all_gather(w_proj, ("dp", "fsdp"), axis=0, tiled=True),
-        lax.all_gather(b_proj, ("dp", "fsdp"), axis=0, tiled=True),
+        lax.all_gather(ln1_gain, AXES, axis=0, tiled=True),
+        lax.all_gather(ln1_bias, AXES, axis=0, tiled=True),
+        lax.all_gather(w_qkv, AXES, axis=0, tiled=True),
+        lax.all_gather(b_qkv, AXES, axis=0, tiled=True),
+        lax.all_gather(w_out, AXES, axis=0, tiled=True),
+        lax.all_gather(b_out, AXES, axis=0, tiled=True),
+        lax.all_gather(ln2_gain, AXES, axis=0, tiled=True),
+        lax.all_gather(ln2_bias, AXES, axis=0, tiled=True),
+        lax.all_gather(w_fc, AXES, axis=0, tiled=True),
+        lax.all_gather(b_fc, AXES, axis=0, tiled=True),
+        lax.all_gather(w_proj, AXES, axis=0, tiled=True),
+        lax.all_gather(b_proj, AXES, axis=0, tiled=True),
     )
     saved = forward(block_input, weight_set, long_flag, fsdp_index, gather_first)
     block_output = saved[0].astype(jnp.bfloat16)
     weight_set = (
-        lax.all_gather(ln1_gain, ("dp", "fsdp"), axis=0, tiled=True),
-        lax.all_gather(ln1_bias, ("dp", "fsdp"), axis=0, tiled=True),
-        lax.all_gather(w_qkv, ("dp", "fsdp"), axis=0, tiled=True),
-        lax.all_gather(b_qkv, ("dp", "fsdp"), axis=0, tiled=True),
-        lax.all_gather(w_out, ("dp", "fsdp"), axis=0, tiled=True),
-        lax.all_gather(b_out, ("dp", "fsdp"), axis=0, tiled=True),
-        lax.all_gather(ln2_gain, ("dp", "fsdp"), axis=0, tiled=True),
-        lax.all_gather(ln2_bias, ("dp", "fsdp"), axis=0, tiled=True),
-        lax.all_gather(w_fc, ("dp", "fsdp"), axis=0, tiled=True),
-        lax.all_gather(b_fc, ("dp", "fsdp"), axis=0, tiled=True),
-        lax.all_gather(w_proj, ("dp", "fsdp"), axis=0, tiled=True),
-        lax.all_gather(b_proj, ("dp", "fsdp"), axis=0, tiled=True),
+        lax.all_gather(ln1_gain, AXES, axis=0, tiled=True),
+        lax.all_gather(ln1_bias, AXES, axis=0, tiled=True),
+        lax.all_gather(w_qkv, AXES, axis=0, tiled=True),
+        lax.all_gather(b_qkv, AXES, axis=0, tiled=True),
+        lax.all_gather(w_out, AXES, axis=0, tiled=True),
+        lax.all_gather(b_out, AXES, axis=0, tiled=True),
+        lax.all_gather(ln2_gain, AXES, axis=0, tiled=True),
+        lax.all_gather(ln2_bias, AXES, axis=0, tiled=True),
+        lax.all_gather(w_fc, AXES, axis=0, tiled=True),
+        lax.all_gather(b_fc, AXES, axis=0, tiled=True),
+        lax.all_gather(w_proj, AXES, axis=0, tiled=True),
+        lax.all_gather(b_proj, AXES, axis=0, tiled=True),
     )
     saved = forward(block_input, weight_set, long_flag, fsdp_index, gather_second)
     input_grad, grad_set = backward(saved, weight_set, block_input, out_grad)
     grad_shards = (
-        lax.psum_scatter(grad_set[0], ("dp", "fsdp"), scatter_dimension=0, tiled=True),
-        lax.psum_scatter(grad_set[1], ("dp", "fsdp"), scatter_dimension=0, tiled=True),
-        lax.psum_scatter(grad_set[2], ("dp", "fsdp"), scatter_dimension=0, tiled=True),
-        lax.psum_scatter(grad_set[3], ("dp", "fsdp"), scatter_dimension=0, tiled=True),
-        lax.psum_scatter(grad_set[4], ("dp", "fsdp"), scatter_dimension=0, tiled=True),
-        lax.psum_scatter(grad_set[5], ("dp", "fsdp"), scatter_dimension=0, tiled=True),
-        lax.psum_scatter(grad_set[6], ("dp", "fsdp"), scatter_dimension=0, tiled=True),
-        lax.psum_scatter(grad_set[7], ("dp", "fsdp"), scatter_dimension=0, tiled=True),
-        lax.psum_scatter(grad_set[8], ("dp", "fsdp"), scatter_dimension=0, tiled=True),
-        lax.psum_scatter(grad_set[9], ("dp", "fsdp"), scatter_dimension=0, tiled=True),
-        lax.psum_scatter(grad_set[10], ("dp", "fsdp"), scatter_dimension=0, tiled=True),
-        lax.psum_scatter(grad_set[11], ("dp", "fsdp"), scatter_dimension=0, tiled=True),
+        lax.psum_scatter(grad_set[0], AXES, scatter_dimension=0, tiled=True),
+        lax.psum_scatter(grad_set[1], AXES, scatter_dimension=0, tiled=True),
+        lax.psum_scatter(grad_set[2], AXES, scatter_dimension=0, tiled=True),
+        lax.psum_scatter(grad_set[3], AXES, scatter_dimension=0, tiled=True),
+        lax.psum_scatter(grad_set[4], AXES, scatter_dimension=0, tiled=True),
+        lax.psum_scatter(grad_set[5], AXES, scatter_dimension=0, tiled=True),
+        lax.psum_scatter(grad_set[6], AXES, scatter_dimension=0, tiled=True),
+        lax.psum_scatter(grad_set[7], AXES, scatter_dimension=0, tiled=True),
+        lax.psum_scatter(grad_set[8], AXES, scatter_dimension=0, tiled=True),
+        lax.psum_scatter(grad_set[9], AXES, scatter_dimension=0, tiled=True),
+        lax.psum_scatter(grad_set[10], AXES, scatter_dimension=0, tiled=True),
+        lax.psum_scatter(grad_set[11], AXES, scatter_dimension=0, tiled=True),
     )
     return (block_output, input_grad) + tuple(grad_shards)
 
@@ -407,7 +407,9 @@
     )
 
 
-def attend_fwd_kernel(block, strips, flag_ref, q_ref, k_ref, v_ref, o_ref, lse_ref, vt_ref):
+def attend_fwd_kernel(
+    block, strips, flag_ref, place_ref, q_ref, k_ref, v_ref, o_ref, send_ref, lse_ref, vt_ref
+):
     i = pl.program_id(0)
     part = block // strips
 
@@ -468,31 +470,38 @@
         top, total, _ = states[h]
         lse_ref[h : h + 1, :] = top + jnp.log(total)
     both = jnp.concatenate([states[h][2] / states[h][1] for h in range(2)], axis=0)
-    o_ref[...] = both.T.astype(bf)
-
-
-def attend_fwd(flag, projected, pair, block=1024, strips=4):
+    heads = both.T.astype(bf)
+    o_ref[...] = heads
+
+    @pl.when(i // (pl.num_programs(0) // 2) != place_ref[0])
+    def _():
+        send_ref[pl.ds(pl.multiple_of(i % (pl.num_programs(0) // 2) * block, block), block), :] = heads
+
+
+def attend_fwd(flag, place, projected, pair, block=1024, strips=4):
     rows = projected.shape[0]
-    full = lambda c: pl.BlockSpec((rows, PAIR), lambda i, f: (0, 3 * pair + c))
+    full = lambda c: pl.BlockSpec((rows, PAIR), lambda i, f, s: (0, 3 * pair + c))
     return pl.pallas_call(
         functools.partial(attend_fwd_kernel, block, strips),
         grid_spec=pltpu.PrefetchScalarGridSpec(
-            num_scalar_prefetch=1,
+            num_scalar_prefetch=2,
             grid=(rows // block,),
-            in_specs=[pl.BlockSpec((block, PAIR), lambda i, f: (i, 3 * pair)), full(1), full(2)],
+            in_specs=[pl.BlockSpec((block, PAIR), lambda i, f, s: (i, 3 * pair)), full(1), full(2)],
             out_specs=[
-                pl.BlockSpec((block, PAIR), lambda i, f: (i, 0)),
-                pl.BlockSpec((8, block), lambda i, f: (0, i)),
+                pl.BlockSpec((block, PAIR), lambda i, f, s: (i, 0)),
+                pl.BlockSpec((rows // 2, PAIR), lambda i, f, s: (0, 0)),
+                pl.BlockSpec((8, block), lambda i, f, s: (0, i)),
             ],
             scratch_shapes=[pltpu.VMEM((PAIR, rows), bf)],
         ),
         out_shape=[
             jax.ShapeDtypeStruct((rows, PAIR), bf),
+            jax.ShapeDtypeStruct((rows // 2, PAIR), bf),
             jax.ShapeDtypeStruct((8, rows), f32),
         ],
         cost_estimate=busy(16),
         name="attend_fwd",
-    )(flag, projected, projected, projected)
+    )(flag, place, projected, projected, projected)
 
 
 def attend_bwd_kernel(
@@ -508,6 +517,7 @@
     other_ref,
     lse_ref,
     g_ref,
+    send_ref,
     dqt_ref,
     inner_ref,
     do_ref,
@@ -588,6 +598,8 @@
     @pl.when(j == last)
     def _():
         g_ref[:, :PAIR] = (dqt_ref[...] * HD**-0.5).T.astype(bf)
+        theirs = pl.multiple_of((1 - place_ref[0]) * side_rows, side_rows)
+        send_ref[...] = g_ref[pl.ds(theirs, side_rows), :]
 
 
 def attend_bwd(flag, place, projected, pair, heads_out, keep, other, lse, block=1024, strips=4):
@@ -604,18 +616,24 @@
                 part(1),
                 part(2),
                 fixed(rows),
-                fixed(rows // 2),
-                fixed(rows // 2),
+                pl.BlockSpec((rows // 2, PAIR), lambda j, f, s: (0, pair)),
+                pl.BlockSpec((rows // 2, PAIR), lambda j, f, s: (0, pair)),
                 pl.BlockSpec((8, rows), lambda j, f, s: (0, 0)),
             ],
-            out_specs=pl.BlockSpec((rows, 3 * PAIR), lambda j, f, s: (0, 0)),
+            out_specs=[
+                pl.BlockSpec((rows, 3 * PAIR), lambda j, f, s: (0, 0)),
+                pl.BlockSpec((rows // 2, 3 * PAIR), lambda j, f, s: (0, 0)),
+            ],
             scratch_shapes=[
                 pltpu.VMEM((PAIR, rows), f32),
                 pltpu.VMEM((8, rows), f32),
                 pltpu.VMEM((rows, PAIR), bf),
             ],
         ),
-        out_shape=jax.ShapeDtypeStruct((rows, 3 * PAIR), bf),
+        out_shape=[
+            jax.ShapeDtypeStruct((rows, 3 * PAIR), bf),
+            jax.ShapeDtypeStruct((rows // 2, 3 * PAIR), bf),
+        ],
         cost_estimate=busy(25),
         name="attend_bwd",
     )(flag, place, projected, projected, projected, heads_out, keep, other, lse)
@@ -637,17 +655,20 @@
     per_side = pl.num_programs(0) // 2
     is_own = pl.program_id(0) // per_side == place_ref[0]
     rows = jnp.where(is_own, own_ref[...], other_ref[...]).astype(f32)
-    unit, _ = norm_stats(rows)
-    normed = (unit * gain_ref[...] + bias_ref[...]).astype(bf)
-    n_ref[...] = normed
-    for c in range(0, p_ref.shape[1], 3 * PAIR):
-        cols = slice(c, c + 3 * PAIR)
-        part = (nn(normed, w_ref[:, cols]) + b_ref[:, cols]).astype(bf)
-        p_ref[:, c : c + PAIR] = part[:, :PAIR] * jnp.asarray(HD**-0.5, bf)
-        p_ref[:, c + PAIR : c + 3 * PAIR] = part[:, PAIR:]
-
-
-def project(place, own, other, gain, bias, weight, w_bias, block=256):
+    piece = rows.shape[0] // 4
+    for r in range(0, rows.shape[0], piece):
+        here = slice(r, r + piece)
+        unit, _ = norm_stats(rows[here])
+        normed = (unit * gain_ref[...] + bias_ref[...]).astype(bf)
+        n_ref[here, :] = normed
+        for c in range(0, p_ref.shape[1], 3 * PAIR):
+            cols = slice(c, c + 3 * PAIR)
+            part = (nn(normed, w_ref[:, cols]) + b_ref[:, cols]).astype(bf)
+            p_ref[here, c : c + PAIR] = part[:, :PAIR] * jnp.asarray(HD**-0.5, bf)
+            p_ref[here, c + PAIR : c + 3 * PAIR] = part[:, PAIR:]
+
+
+def project(place, own, other, gain, bias, weight, w_bias, block=512):
     rows, width = own.shape
     per_side = rows // block
     cols = weight.shape[1]
@@ -710,12 +731,8 @@
     gp_ref,
     gm_ref,
     gml_ref,
-    keep0_ref,
-    keep1_ref,
-    keep2_ref,
-    send0_ref,
-    send1_ref,
-    send2_ref,
+    keep_ref,
+    send_ref,
     sums_ref,
     w_ref,
     sem,
@@ -741,13 +758,17 @@
 
     @pl.when(i == 0)
     def _():
-        for slot in order:
+        load(order[0]).start()
+        load(order[1]).start()
+        load_proj().start()
+        for slot in order[2:]:
             load(slot).start()
-        load_proj().start()
-        for slot in order:
-            load(slot).wait()
-        load_proj().wait()
         sums_ref[...] = jnp.zeros_like(sums_ref)
+
+    def arrive(copy):
+        @pl.when(i == 0)
+        def _():
+            copy.wait()
 
     def weight(slot):
         return w_ref[slot].reshape(width, width)
@@ -757,6 +778,7 @@
     hb = jnp.concatenate([hb0_ref[...], hb1_ref[...], hb2_ref[...]], axis=1)
     mixed = jnp.concatenate([jnp.where(on_left, ha, hb), jnp.where(on_left, hb, ha)], axis=1)
     mixed_ref[...] = mixed
+    arrive(load(order[0]))
     og_low = og_ref[...]
     og = og_low.astype(f32)
     middle = x_ref[...].astype(f32) + nn(mixed, weight(2 * chunks)) + bout_ref[...]
@@ -767,14 +789,17 @@
     e = jnp.zeros_like(middle)
     for c in range(chunks):
         cols = slice(c * width, (c + 1) * width)
+        arrive(load(order[1 + c]))
         w_fc = weight(chunks + c)
-        w_proj = weight(c)
         pre = nn(n2, w_fc) + bfc_ref[:, cols]
+        if c == 0:
+            arrive(load_proj())
         square = pre * pre
         t = jnp.tanh(GELU_C * pre * (1.0 + 0.044715 * square))
         low_half = 0.5 * (1.0 + t)
         act = (pre * low_half).astype(bf)
         act_ref[:, cols] = act
+        w_proj = weight(c)
         out = out + nn(act, w_proj)
         slope = low_half + 0.5 * pre * (1.0 - t * t) * (
             GELU_C * (1.0 + 3.0 * 0.044715 * square)
@@ -801,12 +826,8 @@
     half = width // 2
     left = gh[:, :half]
     right = gh[:, half:]
-    for p, (keep_ref, send_ref) in enumerate(
-        ((keep0_ref, send0_ref), (keep1_ref, send1_ref), (keep2_ref, send2_ref))
-    ):
-        cols = slice(p * PAIR, (p + 1) * PAIR)
-        keep_ref[...] = jnp.where(on_left, left[:, cols], right[:, cols])
-        send_ref[...] = jnp.where(on_left, right[:, cols], left[:, cols])
+    keep_ref[...] = jnp.where(on_left, left, right)
+    send_ref[...] = jnp.where(on_left, right, left)
 
 
 def mlp(place, gathered, x, og, heads_mine, heads_other, b_out, gain, bias, b_fc, b_proj, block=256):
@@ -841,7 +862,7 @@
                 row(hidden),
                 row(width),
                 row(width),
-                *[row(PAIR)] * 6,
+                *[row(width // 2)] * 2,
                 pl.BlockSpec((8, hidden), lambda i, s: (0, 0)),
             ],
             scratch_shapes=[
@@ -857,7 +878,7 @@
             shape(hidden, bf),
             shape(width, f32),
             shape(width, bf),
-            *[shape(PAIR, bf)] * 6,
+            *[shape(width // 2, bf)] * 2,
             jax.ShapeDtypeStruct((8, hidden), f32),
         ],
         compiler_params=pltpu.CompilerParams(vmem_limit_bytes=56 * 1024 * 1024),
@@ -1045,9 +1066,6 @@
     )(x, grad_middle, e, received, weight_other, gain)
 
 
-AXES = ("dp", "fsdp")
-
-
 def swap(value, bit, total):
     return lax.ppermute(value, AXES, [(i, i ^ bit) for i in range(total)])
 
@@ -1083,9 +1101,8 @@
     return held.reshape((rows,) + whole.shape[1:])
 
 
-def sum_all(vector, total):
-    bits = [1 << b for b in range(total.bit_length() - 1)]
-    for bit in bits[1:] + bits[:1]:
+def sum_all(vector, order, total):
+    for bit in [2 << bit for bit in order] + [1]:
         vector = vector + swap(vector, bit, total)
     return vector
 
@@ -1112,7 +1129,6 @@
     side = lax.axis_index("fsdp")
     flat = lax.axis_index("dp") * 2 + side
     on_left = side == 0
-    row_total = block_input.shape[0]
     half = D // 2
     dp_bits = list(range(dp_size.bit_length() - 1))
     gather_order = dp_bits[1:2] + dp_bits[:1:-1] + dp_bits[:1]
@@ -1129,9 +1145,6 @@
         split = rows_in.reshape(rows_in.shape[0], 3, 2, pairs, PAIR)
         mine = lax.dynamic_index_in_dim(split, which, 2, keepdims=False)
         return jnp.transpose(mine, (0, 2, 1, 3)).reshape(rows_in.shape[0], 3 * half)
-
-    def rows_of(whole, which):
-        return lax.dynamic_slice_in_dim(whole, which * row_total, row_total, axis=0)
 
     small = (ln1_gain, ln1_bias, b_qkv, b_out, ln2_gain, ln2_bias, b_fc, b_proj)
     placed = jnp.concatenate(
@@ -1142,7 +1155,7 @@
             for item in small
         ]
     )
-    gathered = sum_all(placed, total).astype(f32)
+    gathered = sum_all(placed, gather_order, total).astype(f32)
     pieces = []
     start = 0
     for item in small:
@@ -1175,10 +1188,10 @@
     heads_other = []
     log_totals = []
     for p in range(pairs):
-        heads, log_total = attend_fwd(seq_long, projected, p)
+        heads, heads_sent, log_total = attend_fwd(seq_long, place, projected, p)
         heads_mine.append(heads)
         log_totals.append(log_total)
-        heads_other.append(swap(rows_of(heads, 1 - side), 1, total))
+        heads_other.append(swap(heads_sent, 1, total))
     (
         block_output,
         mixed,
@@ -1201,9 +1214,8 @@
         as_row(b_fc),
         as_row(b_proj),
     )
-    grad_keep = rest[:pairs]
-    grad_other = [swap(item, 1, total) for item in rest[pairs : 2 * pairs]]
-    sums = rest[2 * pairs]
+    grad_keep, grad_sent, sums = rest
+    grad_other = swap(grad_sent, 1, total)
     packed_grads = weight_grads(
         hidden_act, grad_pre, out_grad, normed_two, mixed, grad_mid_low, total
     )
@@ -1224,21 +1236,25 @@
     )
     grads = []
     grads_other = []
-    shards = []
+    columns = []
     for p in range(pairs):
-        grad_pair = attend_bwd(
+        grad_pair, pair_sent = attend_bwd(
             seq_long,
             place,
             projected,
             p,
             heads_mine[p],
-            grad_keep[p],
-            grad_other[p],
+            grad_keep,
+            grad_other,
             log_totals[p],
         )
         grads.append(grad_pair)
-        grads_other.append(swap(rows_of(grad_pair, 1 - side), 1, total))
-        shards.append(scatter_dp(product_tn(normed_one, grad_pair), dp_size, scatter_order))
+        grads_other.append(swap(pair_sent, 1, total))
+        columns.append(product_tn(normed_one, grad_pair).astype(bf))
+    shards = [
+        scatter_dp(jnp.concatenate(columns[:-1], axis=1), dp_size, scatter_order),
+        scatter_dp(columns[-1], dp_size, scatter_order),
+    ]
 
     e_partial, norm_one_sums, grad_b_mine = norm_sums(
         place, block_input, other_input, grads, grads_other[:-1], w_mine, w_other
@@ -1269,7 +1285,7 @@
         norm_one_sums[1],
         grad_b_qkv,
     )
-    summed = sum_all(jnp.concatenate(grad_vectors), total)
+    summed = sum_all(jnp.concatenate(grad_vectors), scatter_order, total)
     begin = 0
     vector_shards = []
     for item in grad_vectors:
@@ -1305,40 +1321,14 @@
 
 
 def solution(mesh):
-    in_specs = (
-        P(("dp", "fsdp"), None),
-        P("dp"),
-        P(("dp", "fsdp")),
-        P(("dp", "fsdp")),
-        P(("dp", "fsdp"), None),
-        P(("dp", "fsdp")),
-        P(("dp", "fsdp"), None),
-        P(("dp", "fsdp")),
-        P(("dp", "fsdp")),
-        P(("dp", "fsdp")),
-        P(("dp", "fsdp"), None),
-        P(("dp", "fsdp")),
-        P(("dp", "fsdp"), None),
-        P(("dp", "fsdp")),
-        P(("dp", "fsdp"), None),
-    )
-    out_specs = (
-        P(("dp", "fsdp"), None),
-        P(("dp", "fsdp"), None),
-        P(("dp", "fsdp")),
-        P(("dp", "fsdp")),
-        P(("dp", "fsdp"), None),
-        P(("dp", "fsdp")),
-        P(("dp", "fsdp"), None),
-        P(("dp", "fsdp")),
-        P(("dp", "fsdp")),
-        P(("dp", "fsdp")),
-        P(("dp", "fsdp"), None),
-        P(("dp", "fsdp")),
-        P(("dp", "fsdp"), None),
-        P(("dp", "fsdp")),
-    )
-    whole_slice = dict(mesh=mesh, in_specs=in_specs, out_specs=out_specs, check_vma=False)
+    rows, vector, flags = (P(AXES, None), P(AXES), P("dp"))
+    weights = (vector, vector, rows, vector, rows, vector, vector, vector, rows, vector, rows, vector)
+    whole_slice = dict(
+        mesh=mesh,
+        in_specs=(rows, flags) + weights + (rows,),
+        out_specs=(rows, rows) + weights,
+        check_vma=False,
+    )
     dp_size = mesh.shape["dp"]
     if mesh.shape["fsdp"] != 2 or dp_size < 8 or dp_size & (dp_size - 1):
         return jax.shard_map(on_device_generic, **whole_slice)

time: 480 us -> 472 us (0.983)
  waiting for transfers between devices: 140 us -> 130 us
    ppermute x39 -> x33, waiting for transfers between devices: 140 us -> 130 us  [swap(): return lax.ppermute(value, AXES, [(i, i ^ bit) for i in range(total)])]
    ppermute x39 -> x33, starting transfers between devices: 96.2 us -> 101 us  [swap(): return lax.ppermute(value, AXES, [(i, i ^ bit) for i in range(total)])]
    unnamed x67 -> x55, local copies, waits for them, and re-layouts: 14 us -> 12.5 us
  transfers between devices with their start and end apart: 41 -> 35, of which waited for: 22 -> 18; matrix products, arithmetic and copies ran while one was open for 7% -> 8% of each run, Pallas kernels for 36% -> 37%
where the time goes in v1:
time: 472 us; the launch traced here: 465 us
  Pallas kernels  171 us (36%)
  waiting for transfers between devices  130 us (28%)
  starting transfers between devices  101 us (21%)
  local copies, waits for them, and re-layouts  30.6 us (6%)
  between operations  15.6 us (3%)
  matrix products  12 us (3%)
  other arithmetic  6.21 us (1%)
    ppermute x33, waiting for transfers between devices, swap(): return lax.ppermute(value, AXES, [(i, i ^ bit) for i in range(total)])  130 us
    ppermute x33, starting transfers between devices, swap(): return lax.ppermute(value, AXES, [(i, i ^ bit) for i in range(total)])  101 us
    pallas_call x3, Pallas kernels, attend_bwd(): pl.pallas_call(functools.partial(attend_bwd_kernel, block, strips), grid_...  51.6 us
    pallas_call x1, Pallas kernels, mlp(): pl.pallas_call(mlp_kernel, grid_spec=pltpu.PrefetchScalarGridSpec(num_sca...  38.6 us
    pallas_call x3, Pallas kernels, attend_fwd(): pl.pallas_call(functools.partial(attend_fwd_kernel, block, strips), grid_...  30.4 us
    pallas_call x1, Pallas kernels, weight_grads(): pl.pallas_call(weight_grad_kernel, grid=(slots,), in_specs=[pl.BlockSpec(...  19.2 us
    pallas_call x1, Pallas kernels, norm_sums(): pl.pallas_call(norm_sums_kernel, grid_spec=pltpu.PrefetchScalarGridSpec(n...  14 us
    unnamed x55, local copies, waits for them, and re-layouts  12.5 us
  transfers between devices with their start and end apart: 35, of which 18 were waited for; matrix products, arithmetic and copies ran while one was open for 8% of the time, Pallas kernels for 37%

profile of v1, /device:TPU:0, one launch (start us, length us, event | category | flops | bytes accessed | tf_op | source)
XLA Modules:
  0.0 465.1 jit_solution(11272721384023504495)
XLA Ops:
  27.2 14.9 %collective-permute-done.8 = bf16[1,1,2,1,48,1152]{5,4,3,2,1,0:T(8,128)(2,1)S(1)} collective-permute-done((bf16[1,1,2,1,48,1152]{5,4,3,2,1,0:T(8,128)(2,1)S(1)}, bf16[1,1,2,1,48,1152]{5,4,3,2,1,0:T(8,128)(2,1)S(1)}, u32[]{:S(2)}, u32[]{:S(2)}) %collective-permute-start.8) | collective-permute-done | bytes 221216 | tf_op jit(solution)/shard_map/ppermute | solution.py:1070
  53.6 4.0 collective-permute-done.2
  66.4 53.3 %collective-permute-done.5 = bf16[9984]{0:T(1024)(128)(2,1)S(1)} collective-permute-done((bf16[9984]{0:T(1024)(128)(2,1)S(1)}, bf16[9984]{0:T(1024)(128)(2,1)S(1)}, u32[]{:S(2)}, u32[]{:S(2)}) %collective-permute-start.5) | collective-permute-done | bytes 20000 | tf_op jit(solution)/shard_map/ppermute | solution.py:1070
  123.1 9.8 %norm_project.1 = (bf16[2048,768]{1,0:T(8,128)(2,1)}, bf16[2048,1152]{1,0:T(8,128)(2,1)}) custom-call(s32[1]{0:T(128)} %bitcast.place_ref, bf16[1024,768]{1,0:T(8,128)(2,1)} %x_ref.3, bf16[1024,768]{1,0:T(8,128)(2,1)} %collective-permute-done.other_ref, f32[1,768]{1,0:T(1,128)} %reshape.190.gain_ref, f32[1,768]{1,0:T(1,128)} %reshape.191.bias_ref, ...), custom_call_target="tpu_custom_call" | custom-call | flops 12650000384 | bytes 11000000 | tf_op jit(solution)/shard_map/norm_project/pallas_call | solution.py:676
  132.9 10.1 %attend_fwd.4 = (bf16[2048,128]{1,0:T(8,128)(2,1)}, bf16[1024,128]{1,0:T(8,128)(2,1)}, f32[8,2048]{1,0:T(8,128)}) custom-call(s32[1]{0:T(128)S(6)} %copy.82.flag_ref, s32[1]{0:T(128)} %bitcast.place_ref, bf16[2048,1152]{1,0:T(8,128)(2,1)} %get-tuple-element.44.q_ref.k_ref.v_ref, bf16[2048,1152]{1,0:T(8,128)(2,1)} %get-tuple-element.44.q_ref.k_ref.v_ref, ...), custom_call_target="tpu_custom_call" | custom-call | flops 18400000000 | bytes 16000000 | tf_op jit(solution)/shard_map/attend_fwd/pallas_call | solution.py:484
  144.7 10.4 %attend_fwd.5 = (bf16[2048,128]{1,0:T(8,128)(2,1)}, bf16[1024,128]{1,0:T(8,128)(2,1)}, f32[8,2048]{1,0:T(8,128)}) custom-call(s32[1]{0:T(128)S(6)} %copy.82.flag_ref, s32[1]{0:T(128)} %bitcast.place_ref, bf16[2048,1152]{1,0:T(8,128)(2,1)} %get-tuple-element.44.q_ref.k_ref.v_ref, bf16[2048,1152]{1,0:T(8,128)(2,1)} %get-tuple-element.44.q_ref.k_ref.v_ref, ...), custom_call_target="tpu_custom_call" | custom-call | flops 18400000000 | bytes 16000000 | tf_op jit(solution)/shard_map/attend_fwd/pallas_call | solution.py:484
  155.1 10.0 %attend_fwd.3 = (bf16[2048,128]{1,0:T(8,128)(2,1)}, bf16[1024,128]{1,0:T(8,128)(2,1)}, f32[8,2048]{1,0:T(8,128)}) custom-call(s32[1]{0:T(128)S(6)} %copy.82.flag_ref, s32[1]{0:T(128)} %bitcast.place_ref, bf16[2048,1152]{1,0:T(8,128)(2,1)} %get-tuple-element.44.q_ref.k_ref.v_ref, bf16[2048,1152]{1,0:T(8,128)(2,1)} %get-tuple-element.44.q_ref.k_ref.v_ref, ...), custom_call_target="tpu_custom_call" | custom-call | flops 18400000000 | bytes 16000000 | tf_op jit(solution)/shard_map/attend_fwd/pallas_call | solution.py:484
  170.5 3.9 collective-permute-done.13.hb2_ref
  174.4 5.6 %collective-permute-done.11.hb0_ref = bf16[1024,128]{1,0:T(8,128)(2,1)S(1)} collective-permute-done((bf16[1024,128]{1,0:T(8,128)(2,1)}, bf16[1024,128]{1,0:T(8,128)(2,1)S(1)}, u32[]{:S(2)}, u32[]{:S(2)}) %collective-permute-start.11) | collective-permute-done | bytes 262176 | tf_op jit(solution)/shard_map/ppermute | solution.py:1070
  180.7 38.6 %mlp.1 = (bf16[1024,768]{1,0:T(8,128)(2,1)}, bf16[1024,768]{1,0:T(8,128)(2,1)}, bf16[1024,768]{1,0:T(8,128)(2,1)}, bf16[1024,3072]{1,0:T(8,128)(2,1)}, bf16[1024...) custom-call(s32[1]{0:T(128)} %bitcast.place_ref, ...), custom_call_target="tpu_custom_call" | custom-call | flops 42550001664 | bytes 37000000 | tf_op jit(solution)/shard_map/mlp/pallas_call | solution.py:840
  219.7 19.2 %weight_grads.1 = bf16[32,9,24,768]{3,2,1,0:T(8,128)(2,1)} custom-call(bf16[1024,3072]{1,0:T(8,128)(2,1)} %get-tuple-element.69.act_ref, bf16[1024,3072]{1,0:T(8,128)(2,1)} %get-tuple-element.70.gp_ref, bf16[1024,768]{1,0:T(8,128)(2,1)} %og_ref.3, bf16[1024,768]{1,0:T(8,128)(2,1)} %get-tuple-element.71.n2_ref, ...), custom_call_target="tpu_custom_call" | custom-call | flops 21849999360 | bytes 19000000 | tf_op jit(solution)/shard_map/weight_grads/pallas_call | solution.py:939
  245.4 17.3 %attend_bwd.5 = (bf16[2048,384]{1,0:T(8,128)(2,1)}, bf16[1024,384]{1,0:T(8,128)(2,1)}) custom-call(s32[1]{0:T(128)S(6)} %copy.82.flag_ref, s32[1]{0:T(128)} %bitcast.place_ref, bf16[2048,1152]{1,0:T(8,128)(2,1)} %get-tuple-element.44.q_ref.k_ref.v_ref, bf16[2048,1152]{1,0:T(8,128)(2,1)} %get-tuple-element.44.q_ref.k_ref.v_ref, ...), custom_call_target="tpu_custom_call" | custom-call | flops 28750000128 | bytes 25000000 | tf_op jit(solution)/shard_map/attend_bwd/pallas_call | solution.py:609
  262.7 4.2 convolution_convert_fusion
  267.6 17.2 %attend_bwd.3 = (bf16[2048,384]{1,0:T(8,128)(2,1)}, bf16[1024,384]{1,0:T(8,128)(2,1)}) custom-call(s32[1]{0:T(128)S(6)} %copy.82.flag_ref, s32[1]{0:T(128)} %bitcast.place_ref, bf16[2048,1152]{1,0:T(8,128)(2,1)} %get-tuple-element.44.q_ref.k_ref.v_ref, bf16[2048,1152]{1,0:T(8,128)(2,1)} %get-tuple-element.44.q_ref.k_ref.v_ref, ...), custom_call_target="tpu_custom_call" | custom-call | flops 28750000128 | bytes 25000000 | tf_op jit(solution)/shard_map/attend_bwd/pallas_call | solution.py:609
  284.9 4.0 convolution_convert_fusion.2
  288.9 17.0 %attend_bwd.4 = (bf16[2048,384]{1,0:T(8,128)(2,1)}, bf16[1024,384]{1,0:T(8,128)(2,1)}) custom-call(s32[1]{0:T(128)S(6)} %copy.82.flag_ref, s32[1]{0:T(128)} %bitcast.place_ref, bf16[2048,1152]{1,0:T(8,128)(2,1)} %get-tuple-element.44.q_ref.k_ref.v_ref, bf16[2048,1152]{1,0:T(8,128)(2,1)} %get-tuple-element.44.q_ref.k_ref.v_ref, ...), custom_call_target="tpu_custom_call" | custom-call | flops 28750000128 | bytes 25000000 | tf_op jit(solution)/shard_map/attend_bwd/pallas_call | solution.py:609
  306.0 3.8 convolution_convert_fusion.1
  312.2 46.2 %collective-permute-start.29 = (bf16[2,1,2,1,48,384]{5,4,3,2,1,0:T(8,128)(2,1)S(1)}, bf16[2,1,2,1,48,384]{5,4,3,2,1,0:T(8,128)(2,1)S(1)}, u32[]{:S(2)}, u32[]{:S(2)}) collective-permute-start(bf16[2,1,2,1,48,384]{5,4,3,2,1,0:T(8,128)(2,1)S(1)} %select_convert_fusion.1), channel_id=1, source_target_pairs={{0,8},{1,9},{2,10},{3,11},{4,12},{5,13},{6,14},{7,15},{8,0},{9,1},... | collective-permute-start | bytes 442376 | tf_op jit(solution)/shard_map/ppermute | solution.py:1070
  364.1 11.3 %collective-permute-start.30 = (bf16[1,1,2,1,48,384]{5,4,3,2,1,0:T(8,128)(2,1)S(1)}, bf16[1,1,2,1,48,384]{5,4,3,2,1,0:T(8,128)(2,1)S(1)}, u32[]{:S(2)}, u32[]{:S(2)}) collective-permute-start(bf16[1,1,2,1,48,384]{5,4,3,2,1,0:T(8,128)(2,1)S(1)} %select_convert_fusion.3), channel_id=1, source_target_pairs={{0,16},{1,17},{2,18},{3,19},{4,20},{5,21},{6,22},{7,23},{8,24},{9,... | collective-permute-start | bytes 221192 | tf_op jit(solution)/shard_map/ppermute | solution.py:1070
  378.5 5.3 %collective-permute-done.16.r1_ref = bf16[1024,384]{1,0:T(8,128)(2,1)S(1)} collective-permute-done((bf16[1024,384]{1,0:T(8,128)(2,1)S(1)}, bf16[1024,384]{1,0:T(8,128)(2,1)S(1)}, u32[]{:S(2)}, u32[]{:S(2)}) %collective-permute-start.16) | collective-permute-done | bytes 786464 | tf_op jit(solution)/shard_map/ppermute | solution.py:1070
  384.6 18.4 %collective-permute-done.15.r0_ref = bf16[1024,384]{1,0:T(8,128)(2,1)} collective-permute-done((bf16[1024,384]{1,0:T(8,128)(2,1)S(1)}, bf16[1024,384]{1,0:T(8,128)(2,1)}, u32[]{:S(2)}, u32[]{:S(2)}) %collective-permute-start.15) | collective-permute-done | bytes 786464 | tf_op jit(solution)/shard_map/ppermute | solution.py:1070
  403.0 14.0 %norm_sums.1 = (f32[1024,768]{1,0:T(8,128)}, f32[8,768]{1,0:T(8,128)}, f32[8,1152]{1,0:T(8,128)}) custom-call(s32[1]{0:T(128)} %bitcast.place_ref, bf16[1024,768]{1,0:T(8,128)(2,1)} %x_ref.3, bf16[1024,768]{1,0:T(8,128)(2,1)} %collective-permute-done.other_ref, bf16[2048,384]{1,0:T(8,128)(2,1)} %get-tuple-element.56.g0_ref, ...), custom_call_target="tpu_custom_call" | custom-call | flops 14949999616 | bytes 13000000 | tf_op jit(solution)/shard_map/norm_sums/pallas_call | solution.py:1012
  424.1 5.3 %collective-permute-start.21 = (f32[9984]{0:T(1024)S(1)}, f32[9984]{0:T(1024)S(1)}, u32[]{:S(2)}, u32[]{:S(2)}) collective-permute-start(f32[9984]{0:T(1024)S(1)} %add.140), channel_id=1, source_target_pairs={{0,16},{1,17},{2,18},{3,19},{4,20},{5,21},{6,22},{7,23},{8,24},{9,... | collective-permute-start | bytes 119816 | tf_op jit(solution)/shard_map/ppermute | solution.py:1070
  439.8 7.0 %finish.1 = f32[1024,768]{1,0:T(8,128)} custom-call(bf16[1024,768]{1,0:T(8,128)(2,1)} %x_ref.3, f32[1024,768]{1,0:T(8,128)} %get-tuple-element.52.gm_ref, f32[1024,768]{1,0:T(8,128)} %get-tuple-element.63.e_ref, bf16[1024,384]{1,0:T(8,128)(2,1)} %collective-permute-done.18.r_ref, bf16[768,1152]{1,0:T(8,128)(2,1)} %collective-permute-done.17.wo_ref, ...), custom_call_target="tpu_custom_call" | custom-call | flops 6899999744 | bytes 6000000 | tf_op jit(solution)/shard_map/finish/pallas_call | solution.py:1051
  (227 shorter events, 98.9 us)
Async XLA Ops:
  7.2 172.8 %all-gather.2.cloned.1.call-start = ((), (), s32[]{:S(2)}) async-start(), calls=%async_computation.1 | async-start | bytes 10948608 | tf_op jit(solution)/shard_map/all_gather | solution.py:1176
  12.8 441.5 %reduce-scatter.2.cloned.1.call-start = ((), (), s32[]{:S(2)}) async-start(), calls=%async_computation.2 | async-start | bytes 10948608 | tf_op jit(solution)/shard_map/reduce_scatter | solution.py:1222
  24.1 18.0 %collective-permute-start.8 = (bf16[1,1,2,1,48,1152]{5,4,3,2,1,0:T(8,128)(2,1)S(1)}, bf16[1,1,2,1,48,1152]{5,4,3,2,1,0:T(8,128)(2,1)S(1)}, u32[]{:S(2)}, u32[]{:S(2)}) collective-permute-start(bf16[1,1,2,1,48,1152]{5,4,3,2,1,0:T(8,128)(2,1)S(1)} %pad_maximum_fusion.5), channel_id=1, source_target_pairs={{0,16},{1,17},{2,18},{3,19},{4,20},{5,21},{6,22},{7,23},{8,24},{9,... | collective-permute-start | bytes 663560 | tf_op jit(solution)/shard_map/ppermute | solution.py:1070
  42.2 23.9 %collective-permute-start.9 = (bf16[2,1,2,1,48,1152]{5,4,3,2,1,0:T(8,128)(2,1)S(1)}, bf16[2,1,2,1,48,1152]{5,4,3,2,1,0:T(8,128)(2,1)S(1)}, u32[]{:S(2)}, u32[]{:S(2)}) collective-permute-start(bf16[2,1,2,1,48,1152]{5,4,3,2,1,0:T(8,128)(2,1)S(1)} %pad_maximum_fusion.3), channel_id=1, source_target_pairs={{0,8},{1,9},{2,10},{3,11},{4,12},{5,13},{6,14},{7,15},{8,0},{9,1},... | collective-permute-start | bytes 1327112 | tf_op jit(solution)/shard_map/ppermute | solution.py:1070
  63.3 59.8 %collective-permute-start = (bf16[1024,768]{1,0:T(8,128)(2,1)}, bf16[1024,768]{1,0:T(8,128)(2,1)}, u32[]{:S(2)}, u32[]{:S(2)}) collective-permute-start(bf16[1024,768]{1,0:T(8,128)(2,1)} %x_ref.3), channel_id=1, source_target_pairs={{0,1},{1,0},{2,3},{3,2},{4,5},{5,4},{6,7},{7,6},{8,9},{9,8},{10,11... | collective-permute-start | bytes 4718600 | tf_op jit(solution)/shard_map/ppermute | solution.py:1070
  65.6 54.1 %collective-permute-start.5 = (bf16[9984]{0:T(1024)(128)(2,1)S(1)}, bf16[9984]{0:T(1024)(128)(2,1)S(1)}, u32[]{:S(2)}, u32[]{:S(2)}) collective-permute-start(bf16[9984]{0:T(1024)(128)(2,1)S(1)} %add.135), channel_id=1, source_target_pairs={{0,1},{1,0},{2,3},{3,2},{4,5},{5,4},{6,7},{7,6},{8,9},{9,8},{10,11... | collective-permute-start | bytes 59912 | tf_op jit(solution)/shard_map/ppermute | solution.py:1070
  66.3 55.2 %collective-permute-start.10 = (bf16[2,2,2,1,48,1152]{5,4,3,2,1,0:T(8,128)(2,1)S(1)}, bf16[2,2,2,1,48,1152]{5,4,3,2,1,0:T(8,128)(2,1)S(1)}, u32[]{:S(2)}, u32[]{:S(2)}) collective-permute-start(bf16[2,2,2,1,48,1152]{5,4,3,2,1,0:T(8,128)(2,1)S(1)} %pad_maximum_fusion.2), channel_id=1, source_target_pairs={{0,2},{1,3},{2,0},{3,1},{4,6},{5,7},{6,4},{7,5},{8,10},{9,11},{10,... | collective-permute-start | bytes 2654216 | tf_op jit(solution)/shard_map/ppermute | solution.py:1070
  143.0 27.5 %collective-permute-start.12 = (bf16[1024,128]{1,0:T(8,128)(2,1)}, bf16[1024,128]{1,0:T(8,128)(2,1)S(1)}, u32[]{:S(2)}, u32[]{:S(2)}) collective-permute-start(bf16[1024,128]{1,0:T(8,128)(2,1)} %get-tuple-element.49), channel_id=1, source_target_pairs={{0,1},{1,0},{2,3},{3,2},{4,5},{5,4},{6,7},{7,6},{8,9},{9,8},{10,11... | collective-permute-start | bytes 786440 | tf_op jit(solution)/shard_map/ppermute | solution.py:1070
  165.1 9.2 %collective-permute-start.13 = (bf16[1024,128]{1,0:T(8,128)(2,1)S(1)}, bf16[1024,128]{1,0:T(8,128)(2,1)S(1)}, u32[]{:S(2)}, u32[]{:S(2)}) collective-permute-start(bf16[1024,128]{1,0:T(8,128)(2,1)S(1)} %copy-done.9), channel_id=1, source_target_pairs={{0,1},{1,0},{2,3},{3,2},{4,5},{5,4},{6,7},{7,6},{8,9},{9,8},{10,11... | collective-permute-start | bytes 786440 | tf_op jit(solution)/shard_map/ppermute | solution.py:1070
  165.5 14.5 %collective-permute-start.11 = (bf16[1024,128]{1,0:T(8,128)(2,1)}, bf16[1024,128]{1,0:T(8,128)(2,1)S(1)}, u32[]{:S(2)}, u32[]{:S(2)}) collective-permute-start(bf16[1024,128]{1,0:T(8,128)(2,1)} %get-tuple-element.48), channel_id=1, source_target_pairs={{0,1},{1,0},{2,3},{3,2},{4,5},{5,4},{6,7},{7,6},{8,9},{9,8},{10,11... | collective-permute-start | bytes 786440 | tf_op jit(solution)/shard_map/ppermute | solution.py:1070
  170.2 205.5 %collective-permute-start.17 = (bf16[768,1152]{1,0:T(8,128)(2,1)}, bf16[768,1152]{1,0:T(8,128)(2,1)}, u32[]{:S(2)}, u32[]{:S(2)}) collective-permute-start(bf16[768,1152]{1,0:T(8,128)(2,1)} %bitcast.7.w_ref), channel_id=1, source_target_pairs={{0,1},{1,0},{2,3},{3,2},{4,5},{5,4},{6,7},{7,6},{8,9},{9,8},{10,11... | collective-permute-start | bytes 5308424 | tf_op jit(solution)/shard_map/ppermute | solution.py:1070
  219.3 25.2 %collective-permute-start.14 = (bf16[1024,384]{1,0:T(8,128)(2,1)}, bf16[1024,384]{1,0:T(8,128)(2,1)S(1)}, u32[]{:S(2)}, u32[]{:S(2)}) collective-permute-start(bf16[1024,384]{1,0:T(8,128)(2,1)} %get-tuple-element.54), channel_id=1, source_target_pairs={{0,1},{1,0},{2,3},{3,2},{4,5},{5,4},{6,7},{7,6},{8,9},{9,8},{10,11... | collective-permute-start | bytes 2359304 | tf_op jit(solution)/shard_map/ppermute | solution.py:1070
  267.6 43.5 %collective-permute-start.28 = (bf16[2,2,2,1,48,384]{5,4,3,2,1,0:T(8,128)(2,1)}, bf16[2,2,2,1,48,384]{5,4,3,2,1,0:T(8,128)(2,1)}, u32[]{:S(2)}, u32[]{:S(2)}) collective-permute-start(bf16[2,2,2,1,48,384]{5,4,3,2,1,0:T(8,128)(2,1)} %broadcast_select_fusion.5), channel_id=1, source_target_pairs={{0,2},{1,3},{2,0},{3,1},{4,6},{5,7},{6,4},{7,5},{8,10},{9,11},{10,... | collective-permute-start | bytes 884744 | tf_op jit(solution)/shard_map/ppermute | solution.py:1070
  310.6 53.5 %collective-permute-start.24 = (bf16[2,2,2,1,48,768]{5,4,3,2,1,0:T(8,128)(2,1)S(1)}, bf16[2,2,2,1,48,768]{5,4,3,2,1,0:T(8,128)(2,1)S(1)}, u32[]{:S(2)}, u32[]{:S(2)}) collective-permute-start(bf16[2,2,2,1,48,768]{5,4,3,2,1,0:T(8,128)(2,1)S(1)} %broadcast_select_fusion.2), channel_id=1, source_target_pairs={{0,2},{1,3},{2,0},{3,1},{4,6},{5,7},{6,4},{7,5},{8,10},{9,11},{10,... | collective-permute-start | bytes 1769480 | tf_op jit(solution)/shard_map/ppermute | solution.py:1070
  312.2 50.4 %collective-permute-start.29 = (bf16[2,1,2,1,48,384]{5,4,3,2,1,0:T(8,128)(2,1)S(1)}, bf16[2,1,2,1,48,384]{5,4,3,2,1,0:T(8,128)(2,1)S(1)}, u32[]{:S(2)}, u32[]{:S(2)}) collective-permute-start(bf16[2,1,2,1,48,384]{5,4,3,2,1,0:T(8,128)(2,1)S(1)} %select_convert_fusion.1), channel_id=1, source_target_pairs={{0,8},{1,9},{2,10},{3,11},{4,12},{5,13},{6,14},{7,15},{8,0},{9,1},... | collective-permute-start | bytes 442376 | tf_op jit(solution)/shard_map/ppermute | solution.py:1070
  358.5 25.2 %collective-permute-start.16 = (bf16[1024,384]{1,0:T(8,128)(2,1)S(1)}, bf16[1024,384]{1,0:T(8,128)(2,1)S(1)}, u32[]{:S(2)}, u32[]{:S(2)}) collective-permute-start(bf16[1024,384]{1,0:T(8,128)(2,1)S(1)} %copy-done.3), channel_id=1, source_target_pairs={{0,1},{1,0},{2,3},{3,2},{4,5},{5,4},{6,7},{7,6},{8,9},{9,8},{10,11... | collective-permute-start | bytes 2359304 | tf_op jit(solution)/shard_map/ppermute | solution.py:1070
  360.0 43.0 %collective-permute-start.15 = (bf16[1024,384]{1,0:T(8,128)(2,1)S(1)}, bf16[1024,384]{1,0:T(8,128)(2,1)}, u32[]{:S(2)}, u32[]{:S(2)}) collective-permute-start(bf16[1024,384]{1,0:T(8,128)(2,1)S(1)} %copy-done.2), channel_id=1, source_target_pairs={{0,1},{1,0},{2,3},{3,2},{4,5},{5,4},{6,7},{7,6},{8,9},{9,8},{10,11... | collective-permute-start | bytes 2359304 | tf_op jit(solution)/shard_map/ppermute | solution.py:1070
  362.6 77.2 %collective-permute-start.18 = (bf16[1024,384]{1,0:T(8,128)(2,1)}, bf16[1024,384]{1,0:T(8,128)(2,1)}, u32[]{:S(2)}, u32[]{:S(2)}) collective-permute-start(bf16[1024,384]{1,0:T(8,128)(2,1)} %get-tuple-element.64), channel_id=1, source_target_pairs={{0,1},{1,0},{2,3},{3,2},{4,5},{5,4},{6,7},{7,6},{8,9},{9,8},{10,11... | collective-permute-start | bytes 2359304 | tf_op jit(solution)/shard_map/ppermute | solution.py:1070
  364.1 54.8 %collective-permute-start.30 = (bf16[1,1,2,1,48,384]{5,4,3,2,1,0:T(8,128)(2,1)S(1)}, bf16[1,1,2,1,48,384]{5,4,3,2,1,0:T(8,128)(2,1)S(1)}, u32[]{:S(2)}, u32[]{:S(2)}) collective-permute-start(bf16[1,1,2,1,48,384]{5,4,3,2,1,0:T(8,128)(2,1)S(1)} %select_convert_fusion.3), channel_id=1, source_target_pairs={{0,16},{1,17},{2,18},{3,19},{4,20},{5,21},{6,22},{7,23},{8,24},{9,... | collective-permute-start | bytes 221192 | tf_op jit(solution)/shard_map/ppermute | solution.py:1070
  375.7 53.8 %collective-permute-start.25 = (bf16[2,1,2,1,48,768]{5,4,3,2,1,0:T(8,128)(2,1)S(1)}, bf16[2,1,2,1,48,768]{5,4,3,2,1,0:T(8,128)(2,1)S(1)}, u32[]{:S(2)}, u32[]{:S(2)}) collective-permute-start(bf16[2,1,2,1,48,768]{5,4,3,2,1,0:T(8,128)(2,1)S(1)} %select_convert_fusion), channel_id=1, source_target_pairs={{0,8},{1,9},{2,10},{3,11},{4,12},{5,13},{6,14},{7,15},{8,0},{9,1},... | collective-permute-start | bytes 884744 | tf_op jit(solution)/shard_map/ppermute | solution.py:1070
  420.2 13.2 %collective-permute-start.31 = (bf16[1,1,1,1,48,384]{5,4,3,2,1,0:T(8,128)(2,1)S(1)}, bf16[1,1,1,1,48,384]{5,4,3,2,1,0:T(8,128)(2,1)S(1)}, u32[]{:S(2)}, u32[]{:S(2)}) collective-permute-start(bf16[1,1,1,1,48,384]{5,4,3,2,1,0:T(8,128)(2,1)S(1)} %select_convert_fusion.5), channel_id=1, source_target_pairs={{0,4},{1,5},{2,6},{3,7},{4,0},{5,1},{6,2},{7,3},{8,12},{9,13},{10,... | collective-permute-start | bytes 110600 | tf_op jit(solution)/shard_map/ppermute | solution.py:1070
  429.5 8.6 %collective-permute-start.26 = (bf16[1,1,2,1,48,768]{5,4,3,2,1,0:T(8,128)(2,1)S(1)}, bf16[1,1,2,1,48,768]{5,4,3,2,1,0:T(8,128)(2,1)S(1)}, u32[]{:S(2)}, u32[]{:S(2)}) collective-permute-start(bf16[1,1,2,1,48,768]{5,4,3,2,1,0:T(8,128)(2,1)S(1)} %select_convert_fusion.2), channel_id=1, source_target_pairs={{0,16},{1,17},{2,18},{3,19},{4,20},{5,21},{6,22},{7,23},{8,24},{9,... | collective-permute-start | bytes 442376 | tf_op jit(solution)/shard_map/ppermute | solution.py:1070
  435.9 11.0 %collective-permute-start.23 = (f32[9984]{0:T(1024)S(1)}, f32[9984]{0:T(1024)S(1)}, u32[]{:S(2)}, u32[]{:S(2)}) collective-permute-start(f32[9984]{0:T(1024)S(1)} %add.142), channel_id=1, source_target_pairs={{0,1},{1,0},{2,3},{3,2},{4,5},{5,4},{6,7},{7,6},{8,9},{9,8},{10,11... | collective-permute-start | bytes 119816 | tf_op jit(solution)/shard_map/ppermute | solution.py:1070
  438.2 9.8 %collective-permute-start.27 = (bf16[1,1,1,1,48,768]{5,4,3,2,1,0:T(8,128)(2,1)S(1)}, bf16[1,1,1,1,48,768]{5,4,3,2,1,0:T(8,128)(2,1)S(1)}, u32[]{:S(2)}, u32[]{:S(2)}) collective-permute-start(bf16[1,1,1,1,48,768]{5,4,3,2,1,0:T(8,128)(2,1)S(1)} %select_convert_fusion.4), channel_id=1, source_target_pairs={{0,4},{1,5},{2,6},{3,7},{4,0},{5,1},{6,2},{7,3},{8,12},{9,13},{10,... | collective-permute-start | bytes 221192 | tf_op jit(solution)/shard_map/ppermute | solution.py:1070
  (29 other events, 441.0 us)
Sparse Core Ops, SparseCore 0:
  12.9 118.5 all-gather.1
  239.0 171.9 reduce-scatter.1

commit v2 on v1

--- a/solution.py
+++ b/solution.py
@@ -830,7 +830,7 @@
     send_ref[...] = jnp.where(on_left, right, left)
 
 
-def mlp(place, gathered, x, og, heads_mine, heads_other, b_out, gain, bias, b_fc, b_proj, block=256):
+def mlp(place, gathered, x, og, heads_mine, heads_other, b_out, gain, bias, b_fc, b_proj, block=512):
     rows, width = x.shape
     steps = rows // block
     hidden = b_fc.shape[1]
@@ -1070,12 +1070,13 @@
     return lax.ppermute(value, AXES, [(i, i ^ bit) for i in range(total)])
 
 
-def gather_dp(shard, dp_size, order):
+def gather_dp(shard, dp_size, order, arrivals):
     me = lax.axis_index("dp")
     bits = dp_size.bit_length() - 1
     held = shard.reshape((1,) * bits + shard.shape)
     for bit in order:
         other = swap(held, 2 << bit, 2 * dp_size)
+        arrivals.append(other)
         low = (me >> bit) & 1 == 0
         held = jnp.concatenate(
             [jnp.where(low, held, other), jnp.where(low, other, held)], axis=bits - 1 - bit
@@ -1165,7 +1166,10 @@
 
     other_input = swap(block_input, 1, total)
     received = swap(head_columns(w_qkv, 1 - side), 1, total)
-    w_mine = gather_dp(ordered(head_columns(w_qkv, side), received, 0), dp_size, gather_order)
+    arrivals = [received]
+    w_mine = gather_dp(
+        ordered(head_columns(w_qkv, side), received, 0), dp_size, gather_order, arrivals
+    )
     w_other = swap(w_mine, 1, total)
 
     sub = w_out.shape[0]
@@ -1173,6 +1177,7 @@
     packed = jnp.concatenate(
         [w_proj] + [w_fc[:, c * D : (c + 1) * D] for c in range(chunks)] + [w_out], axis=0
     )
+    packed, _ = lax.optimization_barrier((packed, arrivals[1]))
     gathered_w = lax.all_gather(packed, AXES, axis=0, tiled=True)
     gathered_w = gathered_w.reshape(total, 2 * chunks + 1, sub, D)
 

time: 472 us -> 458 us (0.970)
  starting transfers between devices: 101 us -> 92.3 us
    ppermute x33, starting transfers between devices: 101 us -> 92.2 us  [swap(): return lax.ppermute(value, AXES, [(i, i ^ bit) for i in range(total)])]
    unnamed x55 -> x57, local copies, waits for them, and re-layouts: 12.5 us -> 11.7 us
  transfers between devices with their start and end apart: 35 -> 35, of which waited for: 18 -> 18; matrix products, arithmetic and copies ran while one was open for 8% -> 9% of each run, Pallas kernels for 37% -> 38%
where the time goes in v2:
time: 458 us; the launch traced here: 451 us
  Pallas kernels  169 us (37%)
  waiting for transfers between devices  126 us (28%)
  starting transfers between devices  92.3 us (20%)
  local copies, waits for them, and re-layouts  29.1 us (6%)
  between operations  15.7 us (3%)
  matrix products  12.3 us (3%)
  other arithmetic  6.21 us (1%)
    ppermute x33, waiting for transfers between devices, swap(): return lax.ppermute(value, AXES, [(i, i ^ bit) for i in range(total)])  126 us
    ppermute x33, starting transfers between devices, swap(): return lax.ppermute(value, AXES, [(i, i ^ bit) for i in range(total)])  92.2 us
    pallas_call x3, Pallas kernels, attend_bwd(): pl.pallas_call(functools.partial(attend_bwd_kernel, block, strips), grid_...  51.2 us
    pallas_call x1, Pallas kernels, mlp(): pl.pallas_call(mlp_kernel, grid_spec=pltpu.PrefetchScalarGridSpec(num_sca...  37.7 us
    pallas_call x3, Pallas kernels, attend_fwd(): pl.pallas_call(functools.partial(attend_fwd_kernel, block, strips), grid_...  30.5 us
    pallas_call x1, Pallas kernels, weight_grads(): pl.pallas_call(weight_grad_kernel, grid=(slots,), in_specs=[pl.BlockSpec(...  19.3 us
    pallas_call x1, Pallas kernels, norm_sums(): pl.pallas_call(norm_sums_kernel, grid_spec=pltpu.PrefetchScalarGridSpec(n...  14 us
    dot_general x3, matrix products, product_tn(): lax.dot_general(left, right, (((0,), (0,)), ((), ())), preferred_element_...  12.3 us
  transfers between devices with their start and end apart: 35, of which 18 were waited for; matrix products, arithmetic and copies ran while one was open for 9% of the time, Pallas kernels for 38%

profile of v2, /device:TPU:0, one launch (start us, length us, event | category | flops | bytes accessed | tf_op | source)
XLA Modules:
  0.0 450.8 jit_solution(10806942126557494234)
XLA Ops:
  23.3 8.8 %collective-permute-done.8 = bf16[1,1,2,1,48,1152]{5,4,3,2,1,0:T(8,128)(2,1)S(1)} collective-permute-done((bf16[1,1,2,1,48,1152]{5,4,3,2,1,0:T(8,128)(2,1)S(1)}, bf16[1,1,2,1,48,1152]{5,4,3,2,1,0:T(8,128)(2,1)S(1)}, u32[]{:S(2)}, u32[]{:S(2)}) %collective-permute-start.8) | collective-permute-done | bytes 221216 | tf_op jit(solution)/shard_map/ppermute | solution.py:1070
  42.0 3.8 collective-permute-start.4
  48.6 4.5 %collective-permute-start.5 = (bf16[9984]{0:T(1024)(128)(2,1)S(1)}, bf16[9984]{0:T(1024)(128)(2,1)S(1)}, u32[]{:S(2)}, u32[]{:S(2)}) collective-permute-start(bf16[9984]{0:T(1024)(128)(2,1)S(1)} %add.135), channel_id=1, source_target_pairs={{0,8},{1,9},{2,10},{3,11},{4,12},{5,13},{6,14},{7,15},{8,0},{9,1},... | collective-permute-start | bytes 59912 | tf_op jit(solution)/shard_map/ppermute | solution.py:1070
  59.7 51.3 %collective-permute-done.7 = bf16[9984]{0:T(1024)(128)(2,1)S(1)} collective-permute-done((bf16[9984]{0:T(1024)(128)(2,1)S(1)}, bf16[9984]{0:T(1024)(128)(2,1)S(1)}, u32[]{:S(2)}, u32[]{:S(2)}) %collective-permute-start.7) | collective-permute-done | bytes 20000 | tf_op jit(solution)/shard_map/ppermute | solution.py:1070
  114.5 9.7 %norm_project.1 = (bf16[2048,768]{1,0:T(8,128)(2,1)}, bf16[2048,1152]{1,0:T(8,128)(2,1)}) custom-call(s32[1]{0:T(128)} %bitcast.place_ref, bf16[1024,768]{1,0:T(8,128)(2,1)} %x_ref.3, bf16[1024,768]{1,0:T(8,128)(2,1)} %collective-permute-done.2.other_ref, f32[1,768]{1,0:T(1,128)} %reshape.194.gain_ref, f32[1,768]{1,0:T(1,128)} %reshape.195.bias_ref, ...), custom_call_target="tpu_custom_call" | custom-call | flops 12650000384 | bytes 11000000 | tf_op jit(solution)/shard_map/norm_project/pallas_call | solution.py:676
  124.2 10.1 %attend_fwd.4 = (bf16[2048,128]{1,0:T(8,128)(2,1)}, bf16[1024,128]{1,0:T(8,128)(2,1)}, f32[8,2048]{1,0:T(8,128)}) custom-call(s32[1]{0:T(128)S(6)} %copy.82.flag_ref, s32[1]{0:T(128)} %bitcast.place_ref, bf16[2048,1152]{1,0:T(8,128)(2,1)} %get-tuple-element.46.q_ref.k_ref.v_ref, bf16[2048,1152]{1,0:T(8,128)(2,1)} %get-tuple-element.46.q_ref.k_ref.v_ref, ...), custom_call_target="tpu_custom_call" | custom-call | flops 18400000000 | bytes 16000000 | tf_op jit(solution)/shard_map/attend_fwd/pallas_call | solution.py:484
  134.7 10.3 %attend_fwd.5 = (bf16[2048,128]{1,0:T(8,128)(2,1)}, bf16[1024,128]{1,0:T(8,128)(2,1)}, f32[8,2048]{1,0:T(8,128)}) custom-call(s32[1]{0:T(128)S(6)} %copy.82.flag_ref, s32[1]{0:T(128)} %bitcast.place_ref, bf16[2048,1152]{1,0:T(8,128)(2,1)} %get-tuple-element.46.q_ref.k_ref.v_ref, bf16[2048,1152]{1,0:T(8,128)(2,1)} %get-tuple-element.46.q_ref.k_ref.v_ref, ...), custom_call_target="tpu_custom_call" | custom-call | flops 18400000000 | bytes 16000000 | tf_op jit(solution)/shard_map/attend_fwd/pallas_call | solution.py:484
  145.0 10.0 %attend_fwd.3 = (bf16[2048,128]{1,0:T(8,128)(2,1)}, bf16[1024,128]{1,0:T(8,128)(2,1)}, f32[8,2048]{1,0:T(8,128)}) custom-call(s32[1]{0:T(128)S(6)} %copy.82.flag_ref, s32[1]{0:T(128)} %bitcast.place_ref, bf16[2048,1152]{1,0:T(8,128)(2,1)} %get-tuple-element.46.q_ref.k_ref.v_ref, bf16[2048,1152]{1,0:T(8,128)(2,1)} %get-tuple-element.46.q_ref.k_ref.v_ref, ...), custom_call_target="tpu_custom_call" | custom-call | flops 18400000000 | bytes 16000000 | tf_op jit(solution)/shard_map/attend_fwd/pallas_call | solution.py:484
  164.3 5.6 %collective-permute-done.11.hb0_ref = bf16[1024,128]{1,0:T(8,128)(2,1)S(1)} collective-permute-done((bf16[1024,128]{1,0:T(8,128)(2,1)}, bf16[1024,128]{1,0:T(8,128)(2,1)S(1)}, u32[]{:S(2)}, u32[]{:S(2)}) %collective-permute-start.11) | collective-permute-done | bytes 262176 | tf_op jit(solution)/shard_map/ppermute | solution.py:1070
  170.6 37.7 %mlp.1 = (bf16[1024,768]{1,0:T(8,128)(2,1)}, bf16[1024,768]{1,0:T(8,128)(2,1)}, bf16[1024,768]{1,0:T(8,128)(2,1)}, bf16[1024,3072]{1,0:T(8,128)(2,1)}, bf16[1024...) custom-call(s32[1]{0:T(128)} %bitcast.place_ref, ...), custom_call_target="tpu_custom_call" | custom-call | flops 42550001664 | bytes 37000000 | tf_op jit(solution)/shard_map/mlp/pallas_call | solution.py:840
  210.2 19.3 %weight_grads.1 = bf16[32,9,24,768]{3,2,1,0:T(8,128)(2,1)} custom-call(bf16[1024,3072]{1,0:T(8,128)(2,1)} %get-tuple-element.71.act_ref, bf16[1024,3072]{1,0:T(8,128)(2,1)} %get-tuple-element.72.gp_ref, bf16[1024,768]{1,0:T(8,128)(2,1)} %og_ref.3, bf16[1024,768]{1,0:T(8,128)(2,1)} %get-tuple-element.73.n2_ref, ...), custom_call_target="tpu_custom_call" | custom-call | flops 21849999360 | bytes 19000000 | tf_op jit(solution)/shard_map/weight_grads/pallas_call | solution.py:939
  236.0 17.3 %attend_bwd.5 = (bf16[2048,384]{1,0:T(8,128)(2,1)}, bf16[1024,384]{1,0:T(8,128)(2,1)}) custom-call(s32[1]{0:T(128)S(6)} %copy.82.flag_ref, s32[1]{0:T(128)} %bitcast.place_ref, bf16[2048,1152]{1,0:T(8,128)(2,1)} %get-tuple-element.46.q_ref.k_ref.v_ref, bf16[2048,1152]{1,0:T(8,128)(2,1)} %get-tuple-element.46.q_ref.k_ref.v_ref, ...), custom_call_target="tpu_custom_call" | custom-call | flops 28750000128 | bytes 25000000 | tf_op jit(solution)/shard_map/attend_bwd/pallas_call | solution.py:609
  253.3 4.5 convolution_convert_fusion
  258.5 17.0 %attend_bwd.3 = (bf16[2048,384]{1,0:T(8,128)(2,1)}, bf16[1024,384]{1,0:T(8,128)(2,1)}) custom-call(s32[1]{0:T(128)S(6)} %copy.82.flag_ref, s32[1]{0:T(128)} %bitcast.place_ref, bf16[2048,1152]{1,0:T(8,128)(2,1)} %get-tuple-element.46.q_ref.k_ref.v_ref, bf16[2048,1152]{1,0:T(8,128)(2,1)} %get-tuple-element.46.q_ref.k_ref.v_ref, ...), custom_call_target="tpu_custom_call" | custom-call | flops 28750000128 | bytes 25000000 | tf_op jit(solution)/shard_map/attend_bwd/pallas_call | solution.py:609
  275.5 4.0 convolution_convert_fusion.2
  279.5 17.0 %attend_bwd.4 = (bf16[2048,384]{1,0:T(8,128)(2,1)}, bf16[1024,384]{1,0:T(8,128)(2,1)}) custom-call(s32[1]{0:T(128)S(6)} %copy.82.flag_ref, s32[1]{0:T(128)} %bitcast.place_ref, bf16[2048,1152]{1,0:T(8,128)(2,1)} %get-tuple-element.46.q_ref.k_ref.v_ref, bf16[2048,1152]{1,0:T(8,128)(2,1)} %get-tuple-element.46.q_ref.k_ref.v_ref, ...), custom_call_target="tpu_custom_call" | custom-call | flops 28750000128 | bytes 25000000 | tf_op jit(solution)/shard_map/attend_bwd/pallas_call | solution.py:609
  296.5 3.8 convolution_convert_fusion.1
  302.8 44.8 %collective-permute-start.29 = (bf16[2,1,2,1,48,384]{5,4,3,2,1,0:T(8,128)(2,1)S(1)}, bf16[2,1,2,1,48,384]{5,4,3,2,1,0:T(8,128)(2,1)S(1)}, u32[]{:S(2)}, u32[]{:S(2)}) collective-permute-start(bf16[2,1,2,1,48,384]{5,4,3,2,1,0:T(8,128)(2,1)S(1)} %select_convert_fusion.1), channel_id=1, source_target_pairs={{0,8},{1,9},{2,10},{3,11},{4,12},{5,13},{6,14},{7,15},{8,0},{9,1},... | collective-permute-start | bytes 442376 | tf_op jit(solution)/shard_map/ppermute | solution.py:1070
  349.7 7.3 %collective-permute-done.29 = bf16[2,1,2,1,48,384]{5,4,3,2,1,0:T(8,128)(2,1)S(1)} collective-permute-done((bf16[2,1,2,1,48,384]{5,4,3,2,1,0:T(8,128)(2,1)S(1)}, bf16[2,1,2,1,48,384]{5,4,3,2,1,0:T(8,128)(2,1)S(1)}, u32[]{:S(2)}, u32[]{:S(2)}) %collective-permute-start.29) | collective-permute-done | bytes 147488 | tf_op jit(solution)/shard_map/ppermute | solution.py:1070
  363.1 8.6 %collective-permute-done.16.r1_ref = bf16[1024,384]{1,0:T(8,128)(2,1)S(1)} collective-permute-done((bf16[1024,384]{1,0:T(8,128)(2,1)S(1)}, bf16[1024,384]{1,0:T(8,128)(2,1)S(1)}, u32[]{:S(2)}, u32[]{:S(2)}) %collective-permute-start.16) | collective-permute-done | bytes 786464 | tf_op jit(solution)/shard_map/ppermute | solution.py:1070
  372.6 18.4 %collective-permute-done.15.r0_ref = bf16[1024,384]{1,0:T(8,128)(2,1)} collective-permute-done((bf16[1024,384]{1,0:T(8,128)(2,1)S(1)}, bf16[1024,384]{1,0:T(8,128)(2,1)}, u32[]{:S(2)}, u32[]{:S(2)}) %collective-permute-start.15) | collective-permute-done | bytes 786464 | tf_op jit(solution)/shard_map/ppermute | solution.py:1070
  391.0 14.0 %norm_sums.1 = (f32[1024,768]{1,0:T(8,128)}, f32[8,768]{1,0:T(8,128)}, f32[8,1152]{1,0:T(8,128)}) custom-call(s32[1]{0:T(128)} %bitcast.place_ref, bf16[1024,768]{1,0:T(8,128)(2,1)} %x_ref.3, bf16[1024,768]{1,0:T(8,128)(2,1)} %collective-permute-done.2.other_ref, bf16[2048,384]{1,0:T(8,128)(2,1)} %get-tuple-element.58.g0_ref, ...), custom_call_target="tpu_custom_call" | custom-call | flops 14949999616 | bytes 13000000 | tf_op jit(solution)/shard_map/norm_sums/pallas_call | solution.py:1012
  425.4 7.0 %finish.1 = f32[1024,768]{1,0:T(8,128)} custom-call(bf16[1024,768]{1,0:T(8,128)(2,1)} %x_ref.3, f32[1024,768]{1,0:T(8,128)} %get-tuple-element.54.gm_ref, f32[1024,768]{1,0:T(8,128)} %get-tuple-element.65.e_ref, bf16[1024,384]{1,0:T(8,128)(2,1)} %collective-permute-done.18.r_ref, bf16[768,1152]{1,0:T(8,128)(2,1)} %collective-permute-done.17.wo_ref, ...), custom_call_target="tpu_custom_call" | custom-call | flops 6899999744 | bytes 6000000 | tf_op jit(solution)/shard_map/finish/pallas_call | solution.py:1051
  435.0 3.5 collective-permute-done.32
  (229 shorter events, 96.7 us)
Async XLA Ops:
  7.2 162.7 %all-gather.2.cloned.1.call-start = ((), (), s32[]{:S(2)}) async-start(), calls=%async_computation.1 | async-start | bytes 10948608 | tf_op jit(solution)/shard_map/all_gather | solution.py:1181
  20.5 419.3 %reduce-scatter.2.cloned.1.call-start = ((), (), s32[]{:S(2)}) async-start(), calls=%async_computation.2 | async-start | bytes 10948608 | tf_op jit(solution)/shard_map/reduce_scatter | solution.py:1227
  20.6 11.4 %collective-permute-start.8 = (bf16[1,1,2,1,48,1152]{5,4,3,2,1,0:T(8,128)(2,1)S(1)}, bf16[1,1,2,1,48,1152]{5,4,3,2,1,0:T(8,128)(2,1)S(1)}, u32[]{:S(2)}, u32[]{:S(2)}) collective-permute-start(bf16[1,1,2,1,48,1152]{5,4,3,2,1,0:T(8,128)(2,1)S(1)} %pad_maximum_fusion.5), channel_id=1, source_target_pairs={{0,16},{1,17},{2,18},{3,19},{4,20},{5,21},{6,22},{7,23},{8,24},{9,... | collective-permute-start | bytes 663560 | tf_op jit(solution)/shard_map/ppermute | solution.py:1070
  32.2 27.2 %collective-permute-start.9 = (bf16[2,1,2,1,48,1152]{5,4,3,2,1,0:T(8,128)(2,1)S(1)}, bf16[2,1,2,1,48,1152]{5,4,3,2,1,0:T(8,128)(2,1)S(1)}, u32[]{:S(2)}, u32[]{:S(2)}) collective-permute-start(bf16[2,1,2,1,48,1152]{5,4,3,2,1,0:T(8,128)(2,1)S(1)} %pad_maximum_fusion.3), channel_id=1, source_target_pairs={{0,8},{1,9},{2,10},{3,11},{4,12},{5,13},{6,14},{7,15},{8,0},{9,1},... | collective-permute-start | bytes 1327112 | tf_op jit(solution)/shard_map/ppermute | solution.py:1070
  56.6 57.9 %collective-permute-start.2 = (bf16[1024,768]{1,0:T(8,128)(2,1)}, bf16[1024,768]{1,0:T(8,128)(2,1)}, u32[]{:S(2)}, u32[]{:S(2)}) collective-permute-start(bf16[1024,768]{1,0:T(8,128)(2,1)} %x_ref.3), channel_id=1, source_target_pairs={{0,1},{1,0},{2,3},{3,2},{4,5},{5,4},{6,7},{7,6},{8,9},{9,8},{10,11... | collective-permute-start | bytes 4718600 | tf_op jit(solution)/shard_map/ppermute | solution.py:1070
  57.8 53.3 %collective-permute-start.7 = (bf16[9984]{0:T(1024)(128)(2,1)S(1)}, bf16[9984]{0:T(1024)(128)(2,1)S(1)}, u32[]{:S(2)}, u32[]{:S(2)}) collective-permute-start(bf16[9984]{0:T(1024)(128)(2,1)S(1)} %add.137), channel_id=1, source_target_pairs={{0,1},{1,0},{2,3},{3,2},{4,5},{5,4},{6,7},{7,6},{8,9},{9,8},{10,11... | collective-permute-start | bytes 59912 | tf_op jit(solution)/shard_map/ppermute | solution.py:1070
  59.6 53.3 %collective-permute-start.10 = (bf16[2,2,2,1,48,1152]{5,4,3,2,1,0:T(8,128)(2,1)S(1)}, bf16[2,2,2,1,48,1152]{5,4,3,2,1,0:T(8,128)(2,1)S(1)}, u32[]{:S(2)}, u32[]{:S(2)}) collective-permute-start(bf16[2,2,2,1,48,1152]{5,4,3,2,1,0:T(8,128)(2,1)S(1)} %pad_maximum_fusion.2), channel_id=1, source_target_pairs={{0,2},{1,3},{2,0},{3,1},{4,6},{5,7},{6,4},{7,5},{8,10},{9,11},{10,... | collective-permute-start | bytes 2654216 | tf_op jit(solution)/shard_map/ppermute | solution.py:1070
  134.3 27.5 %collective-permute-start.12 = (bf16[1024,128]{1,0:T(8,128)(2,1)}, bf16[1024,128]{1,0:T(8,128)(2,1)S(1)}, u32[]{:S(2)}, u32[]{:S(2)}) collective-permute-start(bf16[1024,128]{1,0:T(8,128)(2,1)} %get-tuple-element.51), channel_id=1, source_target_pairs={{0,1},{1,0},{2,3},{3,2},{4,5},{5,4},{6,7},{7,6},{8,9},{9,8},{10,11... | collective-permute-start | bytes 786440 | tf_op jit(solution)/shard_map/ppermute | solution.py:1070
  155.1 9.2 %collective-permute-start.13 = (bf16[1024,128]{1,0:T(8,128)(2,1)S(1)}, bf16[1024,128]{1,0:T(8,128)(2,1)S(1)}, u32[]{:S(2)}, u32[]{:S(2)}) collective-permute-start(bf16[1024,128]{1,0:T(8,128)(2,1)S(1)} %copy-done.10), channel_id=1, source_target_pairs={{0,1},{1,0},{2,3},{3,2},{4,5},{5,4},{6,7},{7,6},{8,9},{9,8},{10,11... | collective-permute-start | bytes 786440 | tf_op jit(solution)/shard_map/ppermute | solution.py:1070
  156.8 13.1 %collective-permute-start.11 = (bf16[1024,128]{1,0:T(8,128)(2,1)}, bf16[1024,128]{1,0:T(8,128)(2,1)S(1)}, u32[]{:S(2)}, u32[]{:S(2)}) collective-permute-start(bf16[1024,128]{1,0:T(8,128)(2,1)} %get-tuple-element.50), channel_id=1, source_target_pairs={{0,1},{1,0},{2,3},{3,2},{4,5},{5,4},{6,7},{7,6},{8,9},{9,8},{10,11... | collective-permute-start | bytes 786440 | tf_op jit(solution)/shard_map/ppermute | solution.py:1070
  160.1 200.1 %collective-permute-start.17 = (bf16[768,1152]{1,0:T(8,128)(2,1)}, bf16[768,1152]{1,0:T(8,128)(2,1)}, u32[]{:S(2)}, u32[]{:S(2)}) collective-permute-start(bf16[768,1152]{1,0:T(8,128)(2,1)} %bitcast.7.w_ref), channel_id=1, source_target_pairs={{0,1},{1,0},{2,3},{3,2},{4,5},{5,4},{6,7},{7,6},{8,9},{9,8},{10,11... | collective-permute-start | bytes 5308424 | tf_op jit(solution)/shard_map/ppermute | solution.py:1070
  208.3 26.8 %collective-permute-start.14 = (bf16[1024,384]{1,0:T(8,128)(2,1)}, bf16[1024,384]{1,0:T(8,128)(2,1)S(1)}, u32[]{:S(2)}, u32[]{:S(2)}) collective-permute-start(bf16[1024,384]{1,0:T(8,128)(2,1)} %get-tuple-element.56), channel_id=1, source_target_pairs={{0,1},{1,0},{2,3},{3,2},{4,5},{5,4},{6,7},{7,6},{8,9},{9,8},{10,11... | collective-permute-start | bytes 2359304 | tf_op jit(solution)/shard_map/ppermute | solution.py:1070
  258.5 43.2 %collective-permute-start.28 = (bf16[2,2,2,1,48,384]{5,4,3,2,1,0:T(8,128)(2,1)}, bf16[2,2,2,1,48,384]{5,4,3,2,1,0:T(8,128)(2,1)}, u32[]{:S(2)}, u32[]{:S(2)}) collective-permute-start(bf16[2,2,2,1,48,384]{5,4,3,2,1,0:T(8,128)(2,1)} %broadcast_select_fusion.5), channel_id=1, source_target_pairs={{0,2},{1,3},{2,0},{3,1},{4,6},{5,7},{6,4},{7,5},{8,10},{9,11},{10,... | collective-permute-start | bytes 884744 | tf_op jit(solution)/shard_map/ppermute | solution.py:1070
  301.1 56.0 %collective-permute-start.24 = (bf16[2,2,2,1,48,768]{5,4,3,2,1,0:T(8,128)(2,1)S(1)}, bf16[2,2,2,1,48,768]{5,4,3,2,1,0:T(8,128)(2,1)S(1)}, u32[]{:S(2)}, u32[]{:S(2)}) collective-permute-start(bf16[2,2,2,1,48,768]{5,4,3,2,1,0:T(8,128)(2,1)S(1)} %broadcast_select_fusion.2), channel_id=1, source_target_pairs={{0,2},{1,3},{2,0},{3,1},{4,6},{5,7},{6,4},{7,5},{8,10},{9,11},{10,... | collective-permute-start | bytes 1769480 | tf_op jit(solution)/shard_map/ppermute | solution.py:1070
  302.8 54.2 %collective-permute-start.29 = (bf16[2,1,2,1,48,384]{5,4,3,2,1,0:T(8,128)(2,1)S(1)}, bf16[2,1,2,1,48,384]{5,4,3,2,1,0:T(8,128)(2,1)S(1)}, u32[]{:S(2)}, u32[]{:S(2)}) collective-permute-start(bf16[2,1,2,1,48,384]{5,4,3,2,1,0:T(8,128)(2,1)S(1)} %select_convert_fusion.1), channel_id=1, source_target_pairs={{0,8},{1,9},{2,10},{3,11},{4,12},{5,13},{6,14},{7,15},{8,0},{9,1},... | collective-permute-start | bytes 442376 | tf_op jit(solution)/shard_map/ppermute | solution.py:1070
  347.6 24.1 %collective-permute-start.16 = (bf16[1024,384]{1,0:T(8,128)(2,1)S(1)}, bf16[1024,384]{1,0:T(8,128)(2,1)S(1)}, u32[]{:S(2)}, u32[]{:S(2)}) collective-permute-start(bf16[1024,384]{1,0:T(8,128)(2,1)S(1)} %copy-done.4), channel_id=1, source_target_pairs={{0,1},{1,0},{2,3},{3,2},{4,5},{5,4},{6,7},{7,6},{8,9},{9,8},{10,11... | collective-permute-start | bytes 2359304 | tf_op jit(solution)/shard_map/ppermute | solution.py:1070
  348.1 42.9 %collective-permute-start.15 = (bf16[1024,384]{1,0:T(8,128)(2,1)S(1)}, bf16[1024,384]{1,0:T(8,128)(2,1)}, u32[]{:S(2)}, u32[]{:S(2)}) collective-permute-start(bf16[1024,384]{1,0:T(8,128)(2,1)S(1)} %copy-done.3), channel_id=1, source_target_pairs={{0,1},{1,0},{2,3},{3,2},{4,5},{5,4},{6,7},{7,6},{8,9},{9,8},{10,11... | collective-permute-start | bytes 2359304 | tf_op jit(solution)/shard_map/ppermute | solution.py:1070
  357.1 68.4 %collective-permute-start.18 = (bf16[1024,384]{1,0:T(8,128)(2,1)}, bf16[1024,384]{1,0:T(8,128)(2,1)}, u32[]{:S(2)}, u32[]{:S(2)}) collective-permute-start(bf16[1024,384]{1,0:T(8,128)(2,1)} %get-tuple-element.66), channel_id=1, source_target_pairs={{0,1},{1,0},{2,3},{3,2},{4,5},{5,4},{6,7},{7,6},{8,9},{9,8},{10,11... | collective-permute-start | bytes 2359304 | tf_op jit(solution)/shard_map/ppermute | solution.py:1070
  357.1 49.8 %collective-permute-start.30 = (bf16[1,1,2,1,48,384]{5,4,3,2,1,0:T(8,128)(2,1)S(1)}, bf16[1,1,2,1,48,384]{5,4,3,2,1,0:T(8,128)(2,1)S(1)}, u32[]{:S(2)}, u32[]{:S(2)}) collective-permute-start(bf16[1,1,2,1,48,384]{5,4,3,2,1,0:T(8,128)(2,1)S(1)} %select_convert_fusion.3), channel_id=1, source_target_pairs={{0,16},{1,17},{2,18},{3,19},{4,20},{5,21},{6,22},{7,23},{8,24},{9,... | collective-permute-start | bytes 221192 | tf_op jit(solution)/shard_map/ppermute | solution.py:1070
  360.2 54.3 %collective-permute-start.25 = (bf16[2,1,2,1,48,768]{5,4,3,2,1,0:T(8,128)(2,1)S(1)}, bf16[2,1,2,1,48,768]{5,4,3,2,1,0:T(8,128)(2,1)S(1)}, u32[]{:S(2)}, u32[]{:S(2)}) collective-permute-start(bf16[2,1,2,1,48,768]{5,4,3,2,1,0:T(8,128)(2,1)S(1)} %select_convert_fusion), channel_id=1, source_target_pairs={{0,8},{1,9},{2,10},{3,11},{4,12},{5,13},{6,14},{7,15},{8,0},{9,1},... | collective-permute-start | bytes 884744 | tf_op jit(solution)/shard_map/ppermute | solution.py:1070
  409.2 9.4 %collective-permute-start.31 = (bf16[1,1,1,1,48,384]{5,4,3,2,1,0:T(8,128)(2,1)S(1)}, bf16[1,1,1,1,48,384]{5,4,3,2,1,0:T(8,128)(2,1)S(1)}, u32[]{:S(2)}, u32[]{:S(2)}) collective-permute-start(bf16[1,1,1,1,48,384]{5,4,3,2,1,0:T(8,128)(2,1)S(1)} %select_convert_fusion.5), channel_id=1, source_target_pairs={{0,4},{1,5},{2,6},{3,7},{4,0},{5,1},{6,2},{7,3},{8,12},{9,13},{10,... | collective-permute-start | bytes 110600 | tf_op jit(solution)/shard_map/ppermute | solution.py:1070
  414.7 9.1 %collective-permute-start.26 = (bf16[1,1,2,1,48,768]{5,4,3,2,1,0:T(8,128)(2,1)S(1)}, bf16[1,1,2,1,48,768]{5,4,3,2,1,0:T(8,128)(2,1)S(1)}, u32[]{:S(2)}, u32[]{:S(2)}) collective-permute-start(bf16[1,1,2,1,48,768]{5,4,3,2,1,0:T(8,128)(2,1)S(1)} %select_convert_fusion.2), channel_id=1, source_target_pairs={{0,16},{1,17},{2,18},{3,19},{4,20},{5,21},{6,22},{7,23},{8,24},{9,... | collective-permute-start | bytes 442376 | tf_op jit(solution)/shard_map/ppermute | solution.py:1070
  421.1 11.3 %collective-permute-start.23 = (f32[9984]{0:T(1024)S(1)}, f32[9984]{0:T(1024)S(1)}, u32[]{:S(2)}, u32[]{:S(2)}) collective-permute-start(f32[9984]{0:T(1024)S(1)} %add.142), channel_id=1, source_target_pairs={{0,1},{1,0},{2,3},{3,2},{4,5},{5,4},{6,7},{7,6},{8,9},{9,8},{10,11... | collective-permute-start | bytes 119816 | tf_op jit(solution)/shard_map/ppermute | solution.py:1070
  423.9 9.7 %collective-permute-start.27 = (bf16[1,1,1,1,48,768]{5,4,3,2,1,0:T(8,128)(2,1)S(1)}, bf16[1,1,1,1,48,768]{5,4,3,2,1,0:T(8,128)(2,1)S(1)}, u32[]{:S(2)}, u32[]{:S(2)}) collective-permute-start(bf16[1,1,1,1,48,768]{5,4,3,2,1,0:T(8,128)(2,1)S(1)} %select_convert_fusion.4), channel_id=1, source_target_pairs={{0,4},{1,5},{2,6},{3,7},{4,0},{5,1},{6,2},{7,3},{8,12},{9,13},{10,... | collective-permute-start | bytes 221192 | tf_op jit(solution)/shard_map/ppermute | solution.py:1070
  (30 other events, 391.9 us)
Sparse Core Ops, SparseCore 0:
  20.6 110.5 all-gather.1
  229.6 166.9 reduce-scatter.1
